TPU v7x, 256 devices: a whole 4x4x8 slice. The times are simulated.
256 devices in a mesh: seq: 8 (over y, core), doc: 32 (over x, z).
Axes of the slice: x: 4, y: 4, z: 8, core: 2. Of those that a mesh axis runs over, the one named last changes fastest.
Arguments:
- queries: bfloat16 [32, 1024, 2048], P('doc', 'seq'), may hold values from -6 to 6
- keys: bfloat16 [32, 1024, 2048], P('doc', 'seq'), may hold values from -6 to 6
- values: bfloat16 [32, 1024, 2048], P('doc', 'seq'), may hold values from -6 to 6
- w_out: bfloat16 [2048, 2048], P('doc'), may hold values from -0.5 to 0.5
- norm_gain: float32 [2048], replicated, may hold values from 0.1 to 1.9
- w_vocab: bfloat16 [2048, 28672], P(None, 'doc')
- targets: int32 [32, 1024], P('doc', 'seq'), may hold values from 0 to 28671
- domains: int32 [32], replicated, may hold values from 0 to 6, as said below
Outputs:
- projected: bfloat16 [32, 1024, 2048], P('doc', 'seq')
- token_loss: float32 [32, 1024], P('doc', 'seq')
- domain_mean: float32 [7], replicated
Inputs may be any that keep to these rules, and one draw needn't show every extreme that they name: Every one of the 7 domains has at least one document.
All inputs are finite; a program needn't handle non-finite values.
Results may differ from a plain program's by a relative error of at most 0.007.
Values may be sent and summed in bfloat16 or wider, within the bound.
A program may use at most 64 MiB of HBM per device.

v0:
```python
import jax
import jax.numpy as jnp
from jax import lax
from jax.sharding import PartitionSpec as P

HEADS = 16
HD = 128
DOMAINS = 7
BLOCK = 128


def prefix(value, axis, join, neutral):
    count, mine = (lax.axis_size(axis), lax.axis_index(axis))
    pieces = jax.tree.map(lambda part: lax.all_gather(part, axis), value)
    so_far = jax.tree.map(
        lambda part, zero: jnp.full_like(part, 0) + jnp.asarray(zero, part.dtype), value, neutral
    )

    def lap(position, so_far):
        longer = join(so_far, jax.tree.map(lambda part: part[position], pieces))
        return jax.tree.map(lambda new, old: jnp.where(position < mine, new, old), longer, so_far)

    return lax.fori_loop(0, count - 1, lap, so_far)


def combined_all(part, axis, combine):
    gathered = jax.tree.map(lambda a: lax.all_gather(a, axis), part)

    def take(source):
        return jax.tree.map(lambda a: lax.dynamic_index_in_dim(a, source, 0, False), gathered)

    return lax.fori_loop(
        1, lax.axis_size(axis), lambda source, state: combine(state, take(source)), take(0)
    )


def features(inputs):
    return (1.0 + jax.nn.elu(inputs.astype(jnp.float32))).astype(jnp.bfloat16)


def add_pair(earlier, later):
    return (earlier[0] + later[0], earlier[1] + later[1])


def merge_stats(first, second):
    maxima = jnp.maximum(first[0], second[0])
    totals = first[1] * jnp.exp(first[0] - maxima) + second[1] * jnp.exp(second[0] - maxima)
    return (maxima, totals, first[2] + second[2])


def attend_blocks(query_feat, key_feat, value_blk, block_states, block_keys, state_in, sum_in):
    causal = jnp.tril(jnp.ones((BLOCK, BLOCK), dtype=bool))

    def block_step(carry, inputs):
        state, key_sum = carry
        blk_query, blk_key, blk_value, blk_state, blk_keysum = inputs
        scores = jnp.einsum("thf,shf->hts", blk_query, blk_key, preferred_element_type=jnp.float32)
        probs = jnp.where(causal[None], scores, 0.0).astype(jnp.bfloat16)
        numer = jnp.einsum("hts,she->the", probs, blk_value, preferred_element_type=jnp.float32)
        numer = numer + jnp.einsum(
            "thf,hfe->the",
            blk_query,
            state.astype(jnp.bfloat16),
            preferred_element_type=jnp.float32,
        )
        denom = jnp.sum(probs, axis=2, dtype=jnp.float32).T
        denom = denom + jnp.einsum(
            "thf,hf->th", blk_query.astype(jnp.float32), key_sum, precision=lax.Precision.HIGHEST
        )
        outputs = (numer / denom[:, :, None]).astype(jnp.bfloat16)
        return ((state + blk_state, key_sum + blk_keysum), outputs)

    _, outputs = lax.scan(
        block_step, (state_in, sum_in), (query_feat, key_feat, value_blk, block_states, block_keys)
    )
    return outputs


def on_device(queries, keys, values, w_out, norm_gain, w_vocab, targets, domains):
    tokens = queries.shape[1]
    blocks = tokens // BLOCK
    width = HEADS * HD
    query_feat = features(queries[0]).reshape(blocks, BLOCK, HEADS, HD)
    key_feat = features(keys[0]).reshape(blocks, BLOCK, HEADS, HD)
    value_blk = values[0].reshape(blocks, BLOCK, HEADS, HD)
    block_states = jnp.einsum(
        "bshf,bshe->bhfe", key_feat, value_blk, preferred_element_type=jnp.float32
    )
    block_keys = jnp.sum(key_feat, axis=1, dtype=jnp.float32)
    state_local = jnp.sum(block_states, axis=0)
    sum_local = jnp.sum(block_keys, axis=0)
    zero_state = jnp.zeros((HEADS, HD, HD), jnp.float32)
    zero_sum = jnp.zeros((HEADS, HD), jnp.float32)
    state_in, sum_in = prefix((state_local, sum_local), "seq", add_pair, (zero_state, zero_sum))
    attended = attend_blocks(
        query_feat, key_feat, value_blk, block_states, block_keys, state_in, sum_in
    ).reshape(tokens, width)
    projected = jnp.dot(
        attended,
        lax.all_gather(w_out, "doc", axis=0, tiled=True),
        preferred_element_type=jnp.float32,
    ).astype(jnp.bfloat16)
    wide = projected.astype(jnp.float32)
    normed = (
        wide * lax.rsqrt(jnp.mean(wide * wide, axis=-1, keepdims=True) + 1e-05) * norm_gain
    ).astype(jnp.bfloat16)
    vocab_local = w_vocab.shape[1]
    all_targets = lax.all_gather(targets, "doc", axis=0, tiled=True)
    local_ids = all_targets - lax.axis_index("doc") * vocab_local
    vocab_iota = jnp.arange(vocab_local, dtype=jnp.int32)
    logits = jnp.einsum(
        "ntd,dv->ntv",
        lax.all_gather(normed[None], "doc", axis=0, tiled=True),
        w_vocab,
        preferred_element_type=jnp.float32,
    )
    maxima = jnp.max(logits, axis=-1)
    totals = jnp.sum(jnp.exp(logits - maxima[:, :, None]), axis=-1)
    target_hit = jnp.sum(
        jnp.where(vocab_iota[None, None, :] == local_ids[:, :, None], logits, 0.0), axis=-1
    )
    maxima, totals, target_hit = (maxima, totals, target_hit)
    onehot = (domains[:, None] == jnp.arange(DOMAINS, dtype=jnp.int32)[None, :]).astype(jnp.float32)
    top, summed, hits = combined_all((maxima, totals, target_hit), "doc", merge_stats)
    losses = top + jnp.log(summed) - hits
    own_losses = lax.dynamic_slice_in_dim(losses, lax.axis_index("doc"), 1, 0)
    doc_sums = jnp.sum(losses, axis=1)
    partial_sums = jnp.sum(doc_sums[:, None] * onehot, axis=0)
    domain_sums = lax.psum(partial_sums, "seq")
    counts = jnp.sum(onehot, axis=0) * (tokens * lax.axis_size("seq"))
    return (projected[None], own_losses, domain_sums / counts)


def solution(mesh):
    return jax.shard_map(
        on_device,
        mesh=mesh,
        in_specs=(
            P("doc", "seq", None),
            P("doc", "seq", None),
            P("doc", "seq", None),
            P("doc", None),
            P(),
            P(None, "doc"),
            P("doc", "seq"),
            P(),
        ),
        out_specs=(P("doc", "seq", None), P("doc", "seq"), P()),
        check_vma=False,
    )
```

profile of v0, /device:TPU:1, one launch (start us, length us, event | category | flops | bytes accessed | tf_op | source)
XLA Modules:
  0.0 502.8 jit_solution(5402034577404449583)
XLA Ops:
  9.7 1.8 fusion.22
  13.7 1.5 convert_reduce_fusion.1
  15.2 15.8 %all_gather.36 = f32[8,16,128]{2,1,0:T(8,128)S(1)} all-gather(f32[1,16,128]{2,1,0:T(8,128)S(1)} %bitcast.93), channel_id=1, replica_groups=mesh['seq'=8,'doc'=32] {'seq'}, dimensions={0}, use_global_device_ids=true | all-gather | bytes 73728 | tf_op jit(solution)/shard_map/all_gather | solution.py:14
  31.6 1.6 convert_reduce_fusion
  33.2 34.9 %all-gather.12.cloned.1.call-done = f32[128,128,128]{2,1,0:T(8,128)} async-done(((f32[16,128,128]{2,1,0:T(8,128)}), f32[128,128,128]{2,1,0:T(8,128)}) %all-gather.12.cloned.1.call-update) | async-done | bytes 8388624 | tf_op jit(solution)/shard_map/all_gather | solution.py:14
  68.1 11.4 %while.42 = (s32[]{:T(128)}, f32[16,128,128]{2,1,0:T(8,128)S(1)}, f32[16,128]{1,0:T(8,128)S(1)}, s32[]{:T(128)}, f32[8,16,128,128]{3,2,1,0:T(8,128)}, /*index=5*/f32[8,16,128]{2,1,0:T(8,128)S(1)}, s32[]{:T(128)}, s32[]{:T(128)}) while((s32[]{:T(128)}, f32[16,128,128]{2,1,0:T(8,128)S(1)}, f32[16,128]{1,0:T(8,128)S(1)}, s32[]{:T(128)}, ...), condition=%wide.region_2.3_spmd.clone, body=%wide.region_1.2_spmd.clone.sunk | while | flops 792580 | bytes 3170419 | solution.py:23
  68.1 1.6 add_select_fusion.4
  69.7 1.6 add_select_fusion.4
  71.4 1.6 add_select_fusion.4
  73.0 1.6 add_select_fusion.4
  74.6 1.6 add_select_fusion.4
  76.3 1.6 add_select_fusion.4
  77.9 1.6 add_select_fusion.4
  81.4 86.2 %all-gather.10.cloned.1.call-done = bf16[2048,2048]{1,0:T(8,128)(2,1)} async-done(((bf16[64,2048]{1,0:T(8,128)(2,1)}), bf16[2048,2048]{1,0:T(8,128)(2,1)}) %all-gather.10.cloned.1.call-update) | async-done | bytes 8388624 | tf_op jit(solution)/shard_map/all_gather | solution.py:100
  167.6 4.7 fusion.8
  173.4 31.5 %all-gather.5 = s32[32,1,128]{2,1,0:T(1,128)S(1)} all-gather(s32[1,1,128]{2,1,0:T(1,128)S(1)} %bitcast.94), channel_id=1, replica_groups=mesh['seq'=8,'doc'=32] {'doc'}, dimensions={0}, use_global_device_ids=true | all-gather | bytes 16896 | tf_op jit(solution)/shard_map/all_gather | solution.py:108
  204.9 105.4 %all-gather.14.cloned.1.call-done = bf16[4096,2048]{1,0:T(8,128)(2,1)} async-done(((bf16[128,2048]{1,0:T(8,128)(2,1)}), bf16[4096,2048]{1,0:T(8,128)(2,1)}) %all-gather.14.cloned.1.call-update) | async-done | bytes 16777232 | tf_op jit(solution)/shard_map/all_gather | solution.py:113
  310.3 21.6 %fusion.27 = (f32[32,128]{1,0:T(8,128)S(1)}, f32[32,128,896]{2,1,0:T(8,128)S(1)}) fusion(bf16[32,128,2048]{2,1,0:T(8,128)(2,1)} %bitcast.95, bf16[2048,896]{1,0:T(8,128)(2,1)} %param.17), kind=kOutput, calls=%fused_computation.60 | convolution fusion | flops 15036051456 | bytes 35143680 | tf_op jit(solution)/shard_map/ntd,dv->ntv/dot_general | solution.py:111
  331.9 36.1 %all-gather.2 = f32[1024,128]{1,0:T(8,128)S(1)} all-gather(f32[32,128]{1,0:T(8,128)S(1)} %get-tuple-element.386), channel_id=4, replica_groups=mesh['seq'=8,'doc'=32] {'doc'}, dimensions={0}, use_global_device_ids=true | all-gather | bytes 540672 | tf_op jit(solution)/shard_map/all_gather | solution.py:27
  368.0 5.0 select_reduce_fusion
  373.0 35.7 %all-gather.3 = f32[1024,128]{1,0:T(8,128)S(1)} all-gather(f32[32,128]{1,0:T(8,128)S(1)} %get-tuple-element.348), channel_id=5, replica_groups=mesh['seq'=8,'doc'=32] {'doc'}, dimensions={0}, use_global_device_ids=true | all-gather | bytes 540672 | tf_op jit(solution)/shard_map/all_gather | solution.py:27
  408.7 36.0 %all-gather.4 = f32[1024,128]{1,0:T(8,128)S(1)} all-gather(f32[32,128]{1,0:T(8,128)S(1)} %get-tuple-element.347), channel_id=6, replica_groups=mesh['seq'=8,'doc'=32] {'doc'}, dimensions={0}, use_global_device_ids=true | all-gather | bytes 540672 | tf_op jit(solution)/shard_map/all_gather | solution.py:27
  444.7 1.5 while.41
  446.5 48.7 %psum.7 = f32[7]{0:T(128)S(1)} all-reduce(f32[7]{0:T(128)S(1)} %get-tuple-element.350), channel_id=1, replica_groups=mesh['seq'=8,'doc'=32] {'seq'}, use_global_device_ids=true, to_apply=%region_12.13 | all-reduce | flops 7 | bytes 56 | tf_op jit(solution)/shard_map/psum | solution.py:129
  (77 shorter events, 10.2 us)
Async XLA Ops:
  7.2 60.9 %all-gather.12.cloned.1.call-start = ((), (), s32[]{:S(2)}) async-start(), calls=%async_computation.1 | async-start | bytes 9437184 | tf_op jit(solution)/shard_map/all_gather | solution.py:14
  11.5 156.1 %all-gather.10.cloned.1.call-start = ((), (), s32[]{:S(2)}) async-start(), calls=%async_computation | async-start | bytes 8650752 | tf_op jit(solution)/shard_map/all_gather | solution.py:100
  12.3 298.1 %all-gather.14.cloned.1.call-start = ((), (), s32[]{:S(2)}) async-start(), calls=%async_computation.2 | async-start | bytes 17301504 | tf_op jit(solution)/shard_map/all_gather | solution.py:113
  33.2 47.8 %copy-start.4 = (bf16[16,128,128]{1,2,0:T(8,128)(2,1)S(1)}, bf16[16,128,128]{1,2,0:T(8,128)(2,1)}, u32[]{:S(2)}) copy-start(bf16[16,128,128]{1,2,0:T(8,128)(2,1)} %get-tuple-element.383) | copy-start | bytes 1572868
  79.5 92.8 %copy-start.1 = (f32[2048]{0:T(1024)S(1)}, f32[2048]{0:T(1024)}, u32[]{:S(2)}) copy-start(f32[2048]{0:T(1024)} %param.16) | copy-start | bytes 24580
  79.5 93.8 %copy-start.2 = (s32[1,128]{1,0:T(1,128)S(1)}, s32[1,128]{1,0:T(1,128)}, u32[]{:S(2)}) copy-start(s32[1,128]{1,0:T(1,128)} %param.18) | copy-start | bytes 1540
  172.3 159.6 %copy-start = (bf16[128,2048]{1,0:T(8,128)(2,1)}, bf16[128,2048]{1,0:T(8,128)(2,1)S(1)}, u32[]{:S(2)}) copy-start(bf16[128,2048]{1,0:T(8,128)(2,1)S(1)} %get-tuple-element.385) | copy-start | bytes 1572868
  331.9 114.4 %copy-start.3 = (s32[32]{0:T(128)S(1)}, s32[32]{0:T(128)}, u32[]{:S(2)}) copy-start(s32[32]{0:T(128)} %param.19) | copy-start | bytes 388
Sparse Core Ops, SparseCore 0:
  11.6 56.4 all-gather.11
  70.7 96.8 all-gather.9
  173.5 136.7 all-gather.13
where the time goes:
time: 503 us
  waiting for transfers between devices  227 us (45%)
  blocking collectives  204 us (41%)
  matrix products  31.5 us (6%)
  other arithmetic  23.1 us (5%)
  between operations  13.9 us (3%)
    all_gather x3, blocking collectives, combined_all(): gathered = jax.tree.map(lambda a: lax.all_gather(a, axis), part)  108 us
    all_gather x1, waiting for transfers between devices, on_device(): lax.all_gather(normed[None], 'doc', axis=0, tiled=True)  105 us
    all_gather x1, waiting for transfers between devices, on_device(): lax.all_gather(w_out, 'doc', axis=0, tiled=True)  86.2 us
    psum x1, blocking collectives, on_device(): domain_sums = lax.psum(partial_sums, 'seq')  48.7 us
    all_gather x1, waiting for transfers between devices, prefix(): pieces = jax.tree.map(lambda part: lax.all_gather(part, axis), value)  34.9 us
    all_gather x1, blocking collectives, on_device(): all_targets = lax.all_gather(targets, 'doc', axis=0, tiled=True)  31.5 us
    dot_general x1, matrix products, on_device(): jnp.einsum('ntd,dv->ntv', lax.all_gather(normed[None], 'doc', axis=0, til...  21.6 us
    all_gather x1, blocking collectives, prefix(): pieces = jax.tree.map(lambda part: lax.all_gather(part, axis), value)  15.8 us
  transfers between devices with their start and end apart: 3, of which 3 were waited for; matrix products, arithmetic and copies ran while one was open for 4% of the time, Pallas kernels for 0%

commit v1 on v0

--- a/solution.py
+++ b/solution.py
@@ -9,43 +9,8 @@
 BLOCK = 128
 
 
-def prefix(value, axis, join, neutral):
-    count, mine = (lax.axis_size(axis), lax.axis_index(axis))
-    pieces = jax.tree.map(lambda part: lax.all_gather(part, axis), value)
-    so_far = jax.tree.map(
-        lambda part, zero: jnp.full_like(part, 0) + jnp.asarray(zero, part.dtype), value, neutral
-    )
-
-    def lap(position, so_far):
-        longer = join(so_far, jax.tree.map(lambda part: part[position], pieces))
-        return jax.tree.map(lambda new, old: jnp.where(position < mine, new, old), longer, so_far)
-
-    return lax.fori_loop(0, count - 1, lap, so_far)
-
-
-def combined_all(part, axis, combine):
-    gathered = jax.tree.map(lambda a: lax.all_gather(a, axis), part)
-
-    def take(source):
-        return jax.tree.map(lambda a: lax.dynamic_index_in_dim(a, source, 0, False), gathered)
-
-    return lax.fori_loop(
-        1, lax.axis_size(axis), lambda source, state: combine(state, take(source)), take(0)
-    )
-
-
 def features(inputs):
     return (1.0 + jax.nn.elu(inputs.astype(jnp.float32))).astype(jnp.bfloat16)
-
-
-def add_pair(earlier, later):
-    return (earlier[0] + later[0], earlier[1] + later[1])
-
-
-def merge_stats(first, second):
-    maxima = jnp.maximum(first[0], second[0])
-    totals = first[1] * jnp.exp(first[0] - maxima) + second[1] * jnp.exp(second[0] - maxima)
-    return (maxima, totals, first[2] + second[2])
 
 
 def attend_blocks(query_feat, key_feat, value_blk, block_states, block_keys, state_in, sum_in):
@@ -89,9 +54,12 @@
     block_keys = jnp.sum(key_feat, axis=1, dtype=jnp.float32)
     state_local = jnp.sum(block_states, axis=0)
     sum_local = jnp.sum(block_keys, axis=0)
-    zero_state = jnp.zeros((HEADS, HD, HD), jnp.float32)
-    zero_sum = jnp.zeros((HEADS, HD), jnp.float32)
-    state_in, sum_in = prefix((state_local, sum_local), "seq", add_pair, (zero_state, zero_sum))
+    seq_count, seq_mine = (lax.axis_size("seq"), lax.axis_index("seq"))
+    pieces = lax.all_gather(state_local.astype(jnp.bfloat16), "seq")
+    sums = lax.all_gather(sum_local, "seq")
+    earlier = (jnp.arange(seq_count) < seq_mine).astype(jnp.float32)
+    state_in = jnp.sum(pieces.astype(jnp.float32) * earlier[:, None, None, None], axis=0)
+    sum_in = jnp.sum(sums * earlier[:, None, None], axis=0)
     attended = attend_blocks(
         query_feat, key_feat, value_blk, block_states, block_keys, state_in, sum_in
     ).reshape(tokens, width)
@@ -119,14 +87,14 @@
     target_hit = jnp.sum(
         jnp.where(vocab_iota[None, None, :] == local_ids[:, :, None], logits, 0.0), axis=-1
     )
-    maxima, totals, target_hit = (maxima, totals, target_hit)
     onehot = (domains[:, None] == jnp.arange(DOMAINS, dtype=jnp.int32)[None, :]).astype(jnp.float32)
-    top, summed, hits = combined_all((maxima, totals, target_hit), "doc", merge_stats)
-    losses = top + jnp.log(summed) - hits
-    own_losses = lax.dynamic_slice_in_dim(losses, lax.axis_index("doc"), 1, 0)
-    doc_sums = jnp.sum(losses, axis=1)
-    partial_sums = jnp.sum(doc_sums[:, None] * onehot, axis=0)
-    domain_sums = lax.psum(partial_sums, "seq")
+    stats = jnp.stack((maxima, totals, target_hit), axis=1)
+    stats = lax.all_to_all(stats, "doc", 0, 0, tiled=True)
+    top = jnp.max(stats[:, 0], axis=0)
+    summed = jnp.sum(stats[:, 1] * jnp.exp(stats[:, 0] - top[None]), axis=0)
+    own_losses = (top + jnp.log(summed) - jnp.sum(stats[:, 2], axis=0))[None]
+    mine = lax.dynamic_index_in_dim(onehot, lax.axis_index("doc"), 0, False)
+    domain_sums = lax.psum(jnp.sum(own_losses) * mine, ("seq", "doc"))
     counts = jnp.sum(onehot, axis=0) * (tokens * lax.axis_size("seq"))
     return (projected[None], own_losses, domain_sums / counts)
 

time: 503 us -> 419 us (0.83)
  blocking collectives: 204 us -> 123 us
  other arithmetic: 23.1 us -> 16.3 us
  starting transfers between devices: 0.12 us -> 5.47 us
    all_gather x4 -> x1, blocking collectives: 124 us -> 15.8 us  [on_device(): sums = lax.all_gather(sum_local, 'seq')]
    psum x1, blocking collectives: 48.7 us -> 76 us  [on_device(): domain_sums = lax.psum(jnp.sum(own_losses) * mine, ('seq', 'doc'))]
    all_gather x1, waiting for transfers between devices: 34.9 us -> 16.2 us  [on_device(): pieces = lax.all_gather(state_local.astype(jnp.bfloat16), 'seq')]
    select_n x14 -> x0, other arithmetic: 11.2 us -> none  [lap(): jnp.where(position < mine, new, old)]
    all_to_all x0 -> x1, waiting for transfers between devices: none -> 8.78 us  [on_device(): stats = lax.all_to_all(stats, 'doc', 0, 0, tiled=True)]
    all_gather x1, waiting for transfers between devices: 86.2 us -> 94.2 us  [on_device(): lax.all_gather(w_out, 'doc', axis=0, tiled=True)]
    all_to_all x0 -> x1, starting transfers between devices: none -> 5.35 us  [on_device(): stats = lax.all_to_all(stats, 'doc', 0, 0, tiled=True)]
  transfers between devices with their start and end apart: 3 -> 4, of which waited for: 3 -> 4; matrix products, arithmetic and copies ran while one was open for 4% -> 3% of each run, Pallas kernels for 0% -> 0%
where the time goes in v1:
time: 419 us; the launch traced here: 418 us
  waiting for transfers between devices  225 us (54%)
  blocking collectives  123 us (29%)
  matrix products  32.4 us (8%)
  other arithmetic  16.3 us (4%)
  between operations  13.9 us (3%)
  starting transfers between devices  5.47 us (1%)
    all_gather x1, waiting for transfers between devices, on_device(): lax.all_gather(normed[None], 'doc', axis=0, tiled=True)  105 us
    all_gather x1, waiting for transfers between devices, on_device(): lax.all_gather(w_out, 'doc', axis=0, tiled=True)  94.2 us
    psum x1, blocking collectives, on_device(): domain_sums = lax.psum(jnp.sum(own_losses) * mine, ('seq', 'doc'))  76 us
    all_gather x1, blocking collectives, on_device(): all_targets = lax.all_gather(targets, 'doc', axis=0, tiled=True)  31.6 us
    dot_general x1, matrix products, on_device(): jnp.einsum('ntd,dv->ntv', lax.all_gather(normed[None], 'doc', axis=0, til...  21.6 us
    all_gather x1, waiting for transfers between devices, on_device(): pieces = lax.all_gather(state_local.astype(jnp.bfloat16), 'seq')  16.2 us
    all_gather x1, blocking collectives, on_device(): sums = lax.all_gather(sum_local, 'seq')  15.8 us
    all_to_all x1, waiting for transfers between devices, on_device(): stats = lax.all_to_all(stats, 'doc', 0, 0, tiled=True)  8.78 us
  transfers between devices with their start and end apart: 4, of which 4 were waited for; matrix products, arithmetic and copies ran while one was open for 3% of the time, Pallas kernels for 0%

profile of v1, /device:TPU:1, one launch (start us, length us, event | category | flops | bytes accessed | tf_op | source)
XLA Modules:
  0.0 418.3 jit_solution(15200308151373304891)
XLA Ops:
  7.2 1.1 convert_bitcast_fusion
  8.6 1.1 copy.39
  9.7 1.6 convolution_convert_fusion.1
  11.4 0.7 all-gather.7.cloned.1.call-update
  12.1 1.1 convert_bitcast_fusion.1
  13.5 1.5 convert_reduce_fusion
  15.0 15.8 %all_gather.18 = f32[8,16,128]{2,1,0:T(8,128)S(1)} all-gather(f32[1,16,128]{2,1,0:T(8,128)S(1)} %bitcast.81), channel_id=1, replica_groups=mesh['seq'=8,'doc'=32] {'seq'}, dimensions={0}, use_global_device_ids=true | all-gather | bytes 73728 | tf_op jit(solution)/shard_map/all_gather | solution.py:59
  31.5 0.9 fusion.29
  32.4 1.6 convert_reduce_fusion.1
  34.1 16.2 %all-gather.9.cloned.1.call-done = bf16[128,128,128]{2,1,0:T(8,128)(2,1)} async-done(((bf16[16,128,128]{2,1,0:T(8,128)(2,1)}), bf16[128,128,128]{2,1,0:T(8,128)(2,1)}) %all-gather.9.cloned.1.call-update) | async-done | bytes 4194320 | tf_op jit(solution)/shard_map/all_gather | solution.py:58
  50.3 3.1 fusion
  54.0 1.4 fusion.5
  55.4 94.2 %all-gather.7.cloned.1.call-done = bf16[2048,2048]{1,0:T(8,128)(2,1)} async-done(((bf16[64,2048]{1,0:T(8,128)(2,1)}), bf16[2048,2048]{1,0:T(8,128)(2,1)}) %all-gather.7.cloned.1.call-update) | async-done | bytes 8388624 | tf_op jit(solution)/shard_map/all_gather | solution.py:68
  149.6 4.8 %fusion.7 = (f32[128]{0:T(128)S(1)}, bf16[128,2048]{1,0:T(8,128)(2,1)S(1)}) fusion(bf16[128,2048]{0,1:T(8,128)(2,1)S(1)} %bitcast.65, bf16[2048,2048]{1,0:T(8,128)(2,1)} %all-gather.7.cloned.1.call-done), kind=kOutput, calls=%fused_computation.25 | convolution fusion | flops 1074790272 | bytes 9437696 | tf_op jit(solution)/shard_map/dot_general | solution.py:66
  154.3 1.0 fusion.9
  155.4 31.6 %all-gather.2 = s32[32,1,128]{2,1,0:T(1,128)S(1)} all-gather(s32[1,1,128]{2,1,0:T(1,128)S(1)} %bitcast.82), channel_id=1, replica_groups=mesh['seq'=8,'doc'=32] {'doc'}, dimensions={0}, use_global_device_ids=true | all-gather | bytes 16896 | tf_op jit(solution)/shard_map/all_gather | solution.py:76
  187.0 105.3 %all-gather.11.cloned.1.call-done = bf16[4096,2048]{1,0:T(8,128)(2,1)} async-done(((bf16[128,2048]{1,0:T(8,128)(2,1)}), bf16[4096,2048]{1,0:T(8,128)(2,1)}) %all-gather.11.cloned.1.call-update) | async-done | bytes 16777232 | tf_op jit(solution)/shard_map/all_gather | solution.py:81
  292.3 21.6 %fusion.28 = (f32[32,128]{1,0:T(8,128)S(1)}, f32[32,128,896]{2,1,0:T(8,128)S(1)}) fusion(bf16[32,128,2048]{2,1,0:T(8,128)(2,1)} %bitcast.84, bf16[2048,896]{1,0:T(8,128)(2,1)} %param.13), kind=kOutput, calls=%fused_computation.60 | convolution fusion | flops 15036051456 | bytes 35143680 | tf_op jit(solution)/shard_map/ntd,dv->ntv/dot_general | solution.py:79
  313.9 4.5 %exponential_reduce_fusion = (f32[32,128]{1,0:T(8,128)S(1)}, f32[32,128]{1,0:T(8,128)S(1)}) fusion(f32[32,128,896]{2,1,0:T(8,128)S(1)} %get-tuple-element.45, f32[32,128]{1,0:T(8,128)S(1)} %get-tuple-element.44, s32[32,128]{1,0:T(8,128)S(1)} %bitcast.76), kind=kLoop, calls=%fused_computation.2 | loop fusion | flops 18341888 | bytes 14745600 | tf_op jit(solution)/shard_map/reduce_sum | solution.py:86
  318.4 0.7 pad_maximum_fusion
  319.1 5.3 %all-to-all-start = ((f32[32,3,128]{2,1,0:T(4,128)}), f32[32,3,128]{2,1,0:T(4,128)S(1)}, u32[]{:S(2)}, u32[]{:S(2)}) async-start(f32[32,3,128]{2,1,0:T(4,128)} %pad_maximum_fusion), calls=%async_computation | async-start | bytes 131072 | tf_op jit(solution)/shard_map/all_to_all | solution.py:92
  324.5 8.8 %all-to-all-done = f32[32,3,128]{2,1,0:T(4,128)S(1)} async-done(((f32[32,3,128]{2,1,0:T(4,128)}), f32[32,3,128]{2,1,0:T(4,128)S(1)}, u32[]{:S(2)}, u32[]{:S(2)}) %all-to-all-start) | async-done | bytes 49184 | tf_op jit(solution)/shard_map/all_to_all | solution.py:92
  333.4 1.1 fusion.26
  335.3 76.0 %psum.7 = f32[7]{0:T(128)S(1)} all-reduce(f32[7]{0:T(128)S(1)} %multiply_bitcast_fusion), channel_id=1, replica_groups=mesh['seq'=8,'doc'=32] {'seq','doc'}, use_global_device_ids=true, to_apply=%region_12.13 | all-reduce | flops 7 | bytes 56 | tf_op jit(solution)/shard_map/psum | solution.py:97
  (30 shorter events, 3.2 us)
Async XLA Ops:
  7.2 43.1 %all-gather.9.cloned.1.call-start = ((), (), s32[]{:S(2)}) async-start(), calls=%async_computation.2 | async-start | bytes 4718592 | tf_op jit(solution)/shard_map/all_gather | solution.py:58
  11.3 138.2 %all-gather.7.cloned.1.call-start = ((), (), s32[]{:S(2)}) async-start(), calls=%async_computation.1 | async-start | bytes 8650752 | tf_op jit(solution)/shard_map/all_gather | solution.py:68
  12.1 280.2 %all-gather.11.cloned.1.call-start = ((), (), s32[]{:S(2)}) async-start(), calls=%async_computation.3 | async-start | bytes 17301504 | tf_op jit(solution)/shard_map/all_gather | solution.py:81
  34.0 120.3 %copy-start.1 = (f32[2048]{0:T(1024)S(1)}, f32[2048]{0:T(1024)}, u32[]{:S(2)}) copy-start(f32[2048]{0:T(1024)} %param.12) | copy-start | bytes 24580
  50.3 105.1 %copy-start.2 = (s32[1,128]{1,0:T(1,128)S(1)}, s32[1,128]{1,0:T(1,128)}, u32[]{:S(2)}) copy-start(s32[1,128]{1,0:T(1,128)} %param.14) | copy-start | bytes 1540
  154.3 159.6 %copy-start = (bf16[128,2048]{1,0:T(8,128)(2,1)}, bf16[128,2048]{1,0:T(8,128)(2,1)S(1)}, u32[]{:S(2)}) copy-start(bf16[128,2048]{1,0:T(8,128)(2,1)S(1)} %get-tuple-element.43) | copy-start | bytes 1572868
  313.9 10.5 %copy-start.3 = (s32[32]{0:T(128)S(1)}, s32[32]{0:T(128)}, u32[]{:S(2)}) copy-start(s32[32]{0:T(128)} %param.15) | copy-start | bytes 388
  319.1 14.2 %all-to-all-start = ((f32[32,3,128]{2,1,0:T(4,128)}), f32[32,3,128]{2,1,0:T(4,128)S(1)}, u32[]{:S(2)}, u32[]{:S(2)}) async-start(f32[32,3,128]{2,1,0:T(4,128)} %pad_maximum_fusion), calls=%async_computation | async-start | bytes 131072 | tf_op jit(solution)/shard_map/all_to_all | solution.py:92
Sparse Core Ops, SparseCore 0:
  11.4 38.8 all-gather.8
  52.9 96.6 all-gather.6
  155.5 136.7 all-gather.10

commit v2 on v1

--- a/solution.py
+++ b/solution.py
@@ -1,12 +1,450 @@
+import functools
+
 import jax
 import jax.numpy as jnp
 from jax import lax
+from jax.experimental import pallas as pl
+from jax.experimental.pallas import tpu as pltpu
 from jax.sharding import PartitionSpec as P
 
 HEADS = 16
 HD = 128
 DOMAINS = 7
 BLOCK = 128
+D = 2048
+SHARD = 896
+DOCS = 32
+TILE = 256
+NX, NY, NZ = 4, 4, 8
+MESH = pl.DeviceIdType.MESH
+
+
+class Place:
+    def __init__(self):
+        seq, doc = lax.axis_index("seq"), lax.axis_index("doc")
+        self.y, self.c = lax.div(seq, 2), lax.rem(seq, 2)
+        self.x, self.z = lax.div(doc, NZ), lax.rem(doc, NZ)
+        self.pos = self.x * NY + self.y
+
+    def at(self, x=None, y=None, z=None, c=None):
+        x = self.x if x is None else x
+        y = self.y if y is None else y
+        z = self.z if z is None else z
+        c = self.c if c is None else c
+        return {"seq": y * 2 + c, "doc": x * NZ + z}
+
+    def step(self, axis, by):
+        if axis == "x":
+            return self.at(x=lax.rem(self.x + by + NX, NX))
+        if axis == "y":
+            return self.at(y=lax.rem(self.y + by + NY, NY))
+        return self.at(z=lax.rem(self.z + by + NZ, NZ))
+
+    def slot(self, dx, dy):
+        return lax.rem(self.x + dx + NX, NX) * NY + lax.rem(self.y + dy + NY, NY)
+
+    def plane_peer(self, i):
+        other = lax.rem(self.pos + i, NX * NY)
+        return other, self.at(x=lax.div(other, NY), y=lax.rem(other, NY))
+
+    def column_peer(self, i):
+        mine = self.z * 2 + self.c
+        other = lax.rem(mine + i, NZ * 2)
+        return other, self.at(z=lax.div(other, 2), c=lax.rem(other, 2))
+
+
+def remote(src, dst, send, recv, to):
+    return pltpu.make_async_remote_copy(
+        src_ref=src, dst_ref=dst, send_sem=send, recv_sem=recv, device_id=to, device_id_type=MESH
+    )
+
+
+def entry_barrier(here):
+    barrier = pltpu.get_barrier_semaphore()
+
+    def greet(i, _):
+        pl.semaphore_signal(barrier, 1, device_id=here.plane_peer(i)[1], device_id_type=MESH)
+        pl.semaphore_signal(barrier, 1, device_id=here.column_peer(i)[1], device_id_type=MESH)
+        return 0
+
+    lax.fori_loop(1, 16, greet, 0)
+    pl.semaphore_wait(barrier, 30)
+
+
+class VocabRing:
+    def __init__(self, here, w_hbm, wv, near, send, recv, psend, precv):
+        self.here, self.w, self.wv, self.near = here, w_hbm, wv, near
+        self.send, self.recv, self.psend, self.precv = send, recv, psend, precv
+        self.first = pl.multiple_of(here.c * (D // 2), D // 2)
+        self.column = pl.multiple_of(jnp.minimum(here.y * TILE, SHARD - TILE), 128)
+
+    def rows(self, part):
+        if part == "lo":
+            return pl.ds(self.first, D // 4)
+        if part == "hi":
+            return pl.ds(self.first + D // 4, D // 4)
+        return pl.ds(self.first, D // 2)
+
+    def slot(self, off):
+        return lax.rem(self.here.z + off + NZ, NZ)
+
+    def hop(self, k, by, at_receiver):
+        part = "all" if k < 4 else ("lo" if by > 0 else "hi")
+        off = -by * (k if at_receiver else k - 1)
+        dst = self.wv.at[self.slot(off), self.rows(part)]
+        src = self.w.at[self.rows(part), pl.ds(self.column, TILE)] if (k == 1 and not at_receiver) else dst
+        n = 0 if by > 0 else 1
+        return remote(src, dst, self.send.at[n, k - 1], self.recv.at[n, k - 1], self.here.step("z", by))
+
+    def share(self, k, by, at_receiver):
+        part = "all" if k < 4 else ("lo" if by > 0 else "hi")
+        off = -by * k
+        rows = self.rows(part)
+        if at_receiver:
+            start = pl.multiple_of((1 - self.here.c) * (D // 2), D // 2)
+            rows = {"all": pl.ds(start, D // 2), "lo": pl.ds(start, D // 4), "hi": pl.ds(start + D // 4, D // 4)}[part]
+        ref = self.wv.at[self.slot(off), rows]
+        n = 0 if by > 0 else 1
+        return remote(ref, ref, self.psend.at[n, k - 1], self.precv.at[n, k - 1], self.here.at(c=1 - self.here.c))
+
+    def own(self):
+        return pltpu.make_async_copy(self.w.at[:, pl.ds(self.column, TILE)], self.wv.at[self.here.z], self.near)
+
+    def begin(self):
+        for by in (1, -1):
+            self.hop(1, by, False).start()
+        self.own().start()
+
+    def advance(self, k):
+        for by in (1, -1):
+            self.hop(k, by, True).wait_recv()
+            if k < 4:
+                self.hop(k + 1, by, False).start()
+            self.share(k, by, False).start()
+
+    def finish_recv(self):
+        self.own().wait()
+        for k in range(1, 5):
+            for by in (1, -1):
+                self.share(k, by, True).wait_recv()
+
+    def finish_send(self):
+        for k in range(1, 5):
+            for by in (1, -1):
+                self.hop(k, by, False).wait_send()
+                self.share(k, by, False).wait_send()
+
+
+HALF = {
+    "A1+": (0, 0, "all", "A", 1),
+    "A1-": (0, 0, "all", "A", -1),
+    "B1+o": (0, 0, "all", "B", 1),
+    "B1-o": (0, 0, "all", "B", -1),
+    "A2+": (-1, 0, "lo", "A", 1),
+    "A2-": (1, 0, "hi", "A", -1),
+    "B1+m": (-1, 0, "all", "B", 1),
+    "B1-m": (-1, 0, "all", "B", -1),
+    "B1+p": (1, 0, "all", "B", 1),
+    "B1-p": (1, 0, "all", "B", -1),
+    "B1+l": (-2, 0, "lo", "B", 1),
+    "B1-l": (-2, 0, "lo", "B", -1),
+    "B1+h": (2, 0, "hi", "B", 1),
+    "B1-h": (2, 0, "hi", "B", -1),
+    "B2+o": (0, -1, "lo", "B", 1),
+    "B2-o": (0, 1, "hi", "B", -1),
+    "B2+p": (1, -1, "all", "B", 1),
+    "B2-m": (-1, 1, "all", "B", -1),
+    "B2+l": (-2, -1, "lo", "B", 1),
+    "B2-h": (2, 1, "hi", "B", -1),
+}
+ORDER = list(HALF)
+
+
+class PlaneGather:
+    def __init__(self, here, buf, rows, send, recv):
+        self.here, self.buf, self.height, self.send_sem, self.recv_sem = here, buf, rows, send, recv
+
+    def copy(self, half, name, at_receiver):
+        a, b, part, axis, by = HALF[name]
+        if at_receiver:
+            a, b = (a - by, b) if axis == "A" else (a, b - by)
+        first, second = ("x", "y") if half == 0 else ("y", "x")
+        slot = self.here.slot(a, b) if half == 0 else self.here.slot(b, a)
+        unit = self.height // 4
+        row, count = {"all": (0, 2 * unit), "lo": (0, unit), "hi": (unit, unit)}[part]
+        ref = self.buf.at[slot, pl.ds(half * 2 * unit + row, count)]
+        n = half * len(ORDER) + ORDER.index(name)
+        return remote(
+            ref, ref, self.send_sem.at[n], self.recv_sem.at[n], self.here.step(first if axis == "A" else second, by)
+        )
+
+    def send(self, *names):
+        for name in names:
+            for half in (0, 1):
+                self.copy(half, name, False).start()
+
+    def take(self, *names):
+        for name in names:
+            for half in (0, 1):
+                self.copy(half, name, True).wait_recv()
+
+    def begin(self):
+        self.send("A1+", "A1-", "B1+o", "B1-o")
+
+    def event(self, e):
+        if e == 1:
+            self.take("A1+", "A1-")
+            self.send("A2+", "A2-", "B1+m", "B1-m", "B1+p", "B1-p")
+        elif e == 2:
+            self.take("B1+o", "B1-o")
+            self.send("B2+o", "B2-o")
+        elif e == 3:
+            self.take("A2+", "A2-")
+            self.send("B1+l", "B1-l", "B1+h", "B1-h")
+        elif e == 4:
+            self.take("B1+p", "B1-p", "B1+m", "B1-m")
+            self.send("B2+p", "B2-m")
+        elif e == 5:
+            self.take("B2+o", "B2-o")
+        elif e == 6:
+            self.take("B1+l", "B1-l", "B1+h", "B1-h")
+            self.send("B2+l", "B2-h")
+        elif e == 7:
+            self.take("B2+p", "B2-m")
+        else:
+            self.take("B2+l", "B2-h")
+
+    def finish_send(self):
+        for name in ORDER:
+            for half in (0, 1):
+                self.copy(half, name, False).wait_send()
+
+
+SOURCES = (
+    ((0, 0), (-1, 0)),
+    ((1, 0), (0, -1)),
+    ((0, 1), (-1, -1)),
+    ((-1, 1), (1, -1)),
+    ((1, 1), (2, 0)),
+    ((0, 2), (2, -1)),
+    ((2, 1), (-1, 2)),
+    ((1, 2), (2, 2)),
+)
+EVENTS = ((1, 2), (3,), (4,), (), (5,), (6, 7), (), (8,))
+
+
+def pick(table, i):
+    value = table[0]
+    for n in range(1, len(table)):
+        value = jnp.where(i == n, table[n], value)
+    return value
+
+
+def stats_of(here, acts, wv, tcol, p1, p2):
+    rows = 2 * BLOCK
+    lane = lax.broadcasted_iota(jnp.int32, (rows, 128), 1)
+    whole = here.y < NY - 1
+    column = jnp.minimum(here.y * TILE, SHARD - TILE)
+    wanted = jnp.concatenate([tcol[p1], tcol[p2]], axis=0) - lane.astype(jnp.float32)
+
+    def tile(n, carry):
+        top, total, hit = carry
+        left = jnp.concatenate([acts[p1], acts[p2]], axis=0)
+        logits = jnp.dot(left, wv[n], preferred_element_type=jnp.float32)
+        base = ((here.x * NZ + n) * SHARD + column).astype(jnp.float32)
+        one, two = logits[:, :128], logits[:, 128:]
+        now = jnp.maximum(top, jnp.maximum(jnp.where(whole, one, two), two))
+        add = jnp.exp(one - now)
+        total = total * jnp.exp(top - now) + jnp.exp(two - now) + jnp.where(whole, add, 0.0)
+        hit = hit + jnp.where(wanted == jnp.where(whole, base, -1e6), one, 0.0)
+        hit = hit + jnp.where(wanted == base + 128.0, two, 0.0)
+        return now, total, hit
+
+    start = (
+        jnp.full((rows, 128), -jnp.inf, jnp.float32),
+        jnp.zeros((rows, 128), jnp.float32),
+        jnp.zeros((rows, 128), jnp.float32),
+    )
+    top, total, hit = lax.fori_loop(0, NZ, tile, start)
+    peak = jnp.max(top, axis=1, keepdims=True)
+    total = jnp.sum(total * jnp.exp(top - peak), axis=1, keepdims=True)
+    hit = jnp.sum(hit, axis=1, keepdims=True)
+    return jnp.where(lane == 0, peak, jnp.where(lane == 1, total, jnp.where(lane == 2, hit, 0.0)))
+
+
+def vocab_part(here, gather, ring, acts, wv, tg, tcol, out_stats, in_stats, ssend, srecv, tsend, trecv):
+    def columns(slot):
+        wide = jnp.broadcast_to(tg[slot].astype(jnp.float32), (BLOCK, BLOCK))
+        tcol[slot] = wide.T
+
+    def take_targets(i, _):
+        slot, peer = here.plane_peer(i)
+        remote(tg.at[slot], tg.at[slot], tsend.at[i], trecv.at[slot], peer).wait_recv()
+        columns(slot)
+        return 0
+
+    def batch(i, _):
+        for n, events in enumerate(EVENTS):
+            if events or n == 0:
+
+                @pl.when(i == n)
+                def _():
+                    if n == 0:
+                        columns(here.pos)
+                        lax.fori_loop(1, 16, take_targets, 0)
+                    for e in events:
+                        gather.event(e)
+                    if n == 0:
+                        ring.finish_recv()
+
+        slots = []
+        for half in (0, 1):
+            dx = pick([pair[half][0] for pair in SOURCES], i)
+            dy = pick([pair[half][1] for pair in SOURCES], i)
+            slots.append(here.slot(dx, dy))
+        table = stats_of(here, acts, wv, tcol, *slots)
+        for half in (0, 1):
+            slot = slots[half]
+            out_stats[slot] = table[half * BLOCK : (half + 1) * BLOCK].T[:8]
+
+        def give(half):
+            slot = slots[half]
+            to = here.at(x=lax.div(slot, NY), y=lax.rem(slot, NY))
+            remote(out_stats.at[slot], in_stats.at[here.pos], ssend.at[slot], srecv.at[here.pos], to).start()
+
+        @pl.when(i > 0)
+        def _():
+            give(0)
+
+        give(1)
+        return 0
+
+    lax.fori_loop(0, len(SOURCES), batch, 0)
+
+
+def losses_of(here, out_stats, in_stats, ssend, srecv):
+    in_stats[here.pos] = out_stats[here.pos]
+
+    def take(i, _):
+        slot, peer = here.plane_peer(i)
+        remote(out_stats.at[slot], in_stats.at[slot], ssend.at[slot], srecv.at[slot], peer).wait_recv()
+        return 0
+
+    lax.fori_loop(1, 16, take, 0)
+    stats = [in_stats[n] for n in range(16)]
+    top = functools.reduce(jnp.maximum, [s[0:1] for s in stats])
+    total = sum(s[1:2] * jnp.exp(s[0:1] - top) for s in stats)
+    hit = sum(s[2:3] for s in stats)
+    return top + jnp.log(total) - hit
+
+
+def domain_part(here, losses, domains, dom, dsend, drecv):
+    lane = lax.broadcasted_iota(jnp.int32, (8, 128), 1)
+    mine = domains[here.x * NZ + here.z]
+    value = jnp.broadcast_to(jnp.sum(losses, axis=1, keepdims=True), (8, 128))
+    value = jnp.where(lane == mine, value, 0.0)
+    for stage in (0, 1):
+        peers = here.plane_peer if stage == 0 else here.column_peer
+        own = here.pos if stage == 0 else here.z * 2 + here.c
+        dom[stage, own] = value
+
+        def give(i, _):
+            slot, peer = peers(i)
+            remote(dom.at[stage, own], dom.at[stage, own], dsend.at[stage, i], drecv.at[stage, own], peer).start()
+            return 0
+
+        def take(i, _):
+            slot, peer = peers(i)
+            remote(dom.at[stage, slot], dom.at[stage, slot], dsend.at[stage, i], drecv.at[stage, slot], peer).wait_recv()
+            return 0
+
+        lax.fori_loop(1, 16, give, 0)
+        lax.fori_loop(1, 16, take, 0)
+        value = sum(dom[stage, n] for n in range(16))
+    counts = jnp.zeros((8, 128), jnp.float32)
+    for n in range(DOCS):
+        counts = counts + jnp.where(lane == domains[n], 1.0, 0.0)
+    return value / jnp.maximum(counts * (NY * 2 * BLOCK), 1.0)
+
+
+def finish_sends(here, out_stats, in_stats, ssend, srecv, tg, tsend, trecv, dom, dsend, drecv):
+    def one(i, _):
+        slot, peer = here.plane_peer(i)
+        remote(out_stats.at[slot], in_stats.at[slot], ssend.at[slot], srecv.at[slot], peer).wait_send()
+        remote(tg.at[slot], tg.at[slot], tsend.at[i], trecv.at[slot], peer).wait_send()
+        for stage in (0, 1):
+            remote(dom.at[stage, slot], dom.at[stage, slot], dsend.at[stage, i], drecv.at[stage, slot], peer).wait_send()
+        return 0
+
+    lax.fori_loop(1, 16, one, 0)
+
+
+def back_kernel(
+    normed, targets, domains, w_hbm, loss_ref, mean_ref,
+    acts, wv, tg, tcol, out_stats, in_stats, dom,
+    near, gsend, grecv, rsend, rrecv, rpsend, rprecv, tsend, trecv, ssend, srecv, dsend, drecv,
+):
+    here = Place()
+    acts[here.pos] = normed[...]
+    tg[here.pos] = targets[...]
+    entry_barrier(here)
+    ring = VocabRing(here, w_hbm, wv, near, rsend, rrecv, rpsend, rprecv)
+    gather = PlaneGather(here, acts, BLOCK, gsend, grecv)
+    gather.begin()
+    ring.begin()
+
+    def give_targets(i, _):
+        slot, peer = here.plane_peer(i)
+        mine = tg.at[here.pos]
+        remote(mine, mine, tsend.at[i], trecv.at[here.pos], peer).start()
+        return 0
+
+    lax.fori_loop(1, 16, give_targets, 0)
+    for k in range(1, 5):
+        ring.advance(k)
+    vocab_part(here, gather, ring, acts, wv, tg, tcol, out_stats, in_stats, ssend, srecv, tsend, trecv)
+    losses = losses_of(here, out_stats, in_stats, ssend, srecv)
+    loss_ref[...] = losses
+    mean_ref[...] = domain_part(here, losses, domains, dom, dsend, drecv)
+    gather.finish_send()
+    ring.finish_send()
+    finish_sends(here, out_stats, in_stats, ssend, srecv, tg, tsend, trecv, dom, dsend, drecv)
+
+
+def back(normed, targets, domains, w_vocab):
+    vmem = pl.BlockSpec(memory_space=pltpu.VMEM)
+    dma = pltpu.SemaphoreType.DMA
+    return pl.pallas_call(
+        back_kernel,
+        out_shape=(jax.ShapeDtypeStruct((1, BLOCK), jnp.float32), jax.ShapeDtypeStruct((8, 128), jnp.float32)),
+        in_specs=[vmem, vmem, pl.BlockSpec(memory_space=pltpu.SMEM), pl.BlockSpec(memory_space=pl.ANY)],
+        out_specs=(vmem, vmem),
+        scratch_shapes=[
+            pltpu.VMEM((16, BLOCK, D), jnp.bfloat16),
+            pltpu.VMEM((NZ, D, TILE), jnp.bfloat16),
+            pltpu.VMEM((16, 1, BLOCK), jnp.int32),
+            pltpu.VMEM((16, BLOCK, BLOCK), jnp.float32),
+            pltpu.VMEM((16, 8, 128), jnp.float32),
+            pltpu.VMEM((16, 8, 128), jnp.float32),
+            pltpu.VMEM((2, 16, 8, 128), jnp.float32),
+            dma(()),
+            dma((40,)),
+            dma((40,)),
+            dma((2, 4)),
+            dma((2, 4)),
+            dma((2, 4)),
+            dma((2, 4)),
+            dma((16,)),
+            dma((16,)),
+            dma((16,)),
+            dma((16,)),
+            dma((2, 16)),
+            dma((2, 16)),
+        ],
+        compiler_params=pltpu.CompilerParams(
+            collective_id=0, has_side_effects=True, vmem_limit_bytes=60 * 1024 * 1024
+        ),
+    )(normed, targets, domains, w_vocab)
 
 
 def features(inputs):
@@ -72,31 +510,8 @@
     normed = (
         wide * lax.rsqrt(jnp.mean(wide * wide, axis=-1, keepdims=True) + 1e-05) * norm_gain
     ).astype(jnp.bfloat16)
-    vocab_local = w_vocab.shape[1]
-    all_targets = lax.all_gather(targets, "doc", axis=0, tiled=True)
-    local_ids = all_targets - lax.axis_index("doc") * vocab_local
-    vocab_iota = jnp.arange(vocab_local, dtype=jnp.int32)
-    logits = jnp.einsum(
-        "ntd,dv->ntv",
-        lax.all_gather(normed[None], "doc", axis=0, tiled=True),
-        w_vocab,
-        preferred_element_type=jnp.float32,
-    )
-    maxima = jnp.max(logits, axis=-1)
-    totals = jnp.sum(jnp.exp(logits - maxima[:, :, None]), axis=-1)
-    target_hit = jnp.sum(
-        jnp.where(vocab_iota[None, None, :] == local_ids[:, :, None], logits, 0.0), axis=-1
-    )
-    onehot = (domains[:, None] == jnp.arange(DOMAINS, dtype=jnp.int32)[None, :]).astype(jnp.float32)
-    stats = jnp.stack((maxima, totals, target_hit), axis=1)
-    stats = lax.all_to_all(stats, "doc", 0, 0, tiled=True)
-    top = jnp.max(stats[:, 0], axis=0)
-    summed = jnp.sum(stats[:, 1] * jnp.exp(stats[:, 0] - top[None]), axis=0)
-    own_losses = (top + jnp.log(summed) - jnp.sum(stats[:, 2], axis=0))[None]
-    mine = lax.dynamic_index_in_dim(onehot, lax.axis_index("doc"), 0, False)
-    domain_sums = lax.psum(jnp.sum(own_losses) * mine, ("seq", "doc"))
-    counts = jnp.sum(onehot, axis=0) * (tokens * lax.axis_size("seq"))
-    return (projected[None], own_losses, domain_sums / counts)
+    own_losses, means = back(normed, targets, domains, w_vocab)
+    return (projected[None], own_losses, means[0, :DOMAINS])
 
 
 def solution(mesh):

time: 419 us -> 281 us (0.67)
  Pallas kernels: 0 us -> 116 us
  waiting for transfers between devices: 225 us -> 115 us
  blocking collectives: 123 us -> 15.8 us
  matrix products: 32.4 us -> 8.92 us
  other arithmetic: 16.3 us -> 6.59 us
  starting transfers between devices: 5.47 us -> 0.08 us
    pallas_call x0 -> x1, Pallas kernels: none -> 116 us  [back(): pl.pallas_call(back_kernel, out_shape=(jax.ShapeDtypeStruct((1, BLOCK), j...]
    all_gather x1 -> x0, waiting for transfers between devices: 105 us -> none  [on_device(): lax.all_gather(normed[None], 'doc', axis=0, tiled=True)]
    psum x1 -> x0, blocking collectives: 76 us -> none  [on_device(): domain_sums = lax.psum(jnp.sum(own_losses) * mine, ('seq', 'doc'))]
    all_gather x1 -> x0, blocking collectives: 31.6 us -> none  [on_device(): all_targets = lax.all_gather(targets, 'doc', axis=0, tiled=True)]
    dot_general x1 -> x0, matrix products: 21.6 us -> none  [on_device(): jnp.einsum('ntd,dv->ntv', lax.all_gather(normed[None], 'doc', axis=0, til...]
    all_to_all x1 -> x0, waiting for transfers between devices: 8.78 us -> none  [on_device(): stats = lax.all_to_all(stats, 'doc', 0, 0, tiled=True)]
    reduce_sum x4 -> x0, other arithmetic: 5.7 us -> none  [the longest x1 4.46 us: on_device(): totals = jnp.sum(jnp.exp(logits - maxima[:, :, None]), axis=-1)]
    all_to_all x1 -> x0, starting transfers between devices: 5.35 us -> none  [on_device(): stats = lax.all_to_all(stats, 'doc', 0, 0, tiled=True)]
  transfers between devices with their start and end apart: 4 -> 2, of which waited for: 4 -> 2; matrix products, arithmetic and copies ran while one was open for 3% -> 3% of each run, Pallas kernels for 0% -> 0%
where the time goes in v2:
time: 281 us; the launch traced here: 280 us
  Pallas kernels  116 us (41%)
  waiting for transfers between devices  115 us (41%)
  blocking collectives  15.8 us (6%)
  between operations  14.2 us (5%)
  matrix products  8.92 us (3%)
  other arithmetic  6.59 us (2%)
  local copies, waits for them, and re-layouts  3.84 us (1%)
    pallas_call x1, Pallas kernels, back(): pl.pallas_call(back_kernel, out_shape=(jax.ShapeDtypeStruct((1, BLOCK), j...  116 us
    all_gather x1, waiting for transfers between devices, on_device(): lax.all_gather(w_out, 'doc', axis=0, tiled=True)  95.2 us
    all_gather x1, waiting for transfers between devices, on_device(): pieces = lax.all_gather(state_local.astype(jnp.bfloat16), 'seq')  19.2 us
    all_gather x1, blocking collectives, on_device(): sums = lax.all_gather(sum_local, 'seq')  15.8 us
  transfers between devices with their start and end apart: 2, of which 2 were waited for; matrix products, arithmetic and copies ran while one was open for 3% of the time, Pallas kernels for 0%

profile of v2, /device:TPU:1, one launch (start us, length us, event | category | flops | bytes accessed | tf_op | source)
XLA Modules:
  0.0 280.3 jit_solution(490300437498022032)
XLA Ops:
  7.2 1.2 convert_bitcast_fusion
  8.5 0.2 copy.39
  8.7 1.1 copy.37
  9.8 1.6 convolution_convert_fusion.1
  11.4 0.0 all-gather.4.cloned.1.call-start
  11.5 0.7 all-gather.4.cloned.1.call-update
  12.2 0.1 convert_bitcast_fusion.1
  12.3 0.2 copy.38
  12.5 0.5 convert_reduce_fusion
  13.0 15.8 %all_gather.12 = f32[8,16,128]{2,1,0:T(8,128)S(1)} all-gather(f32[1,16,128]{2,1,0:T(8,128)S(1)} %bitcast.54), channel_id=1, replica_groups=mesh['seq'=8,'doc'=32] {'seq'}, dimensions={0}, use_global_device_ids=true | all-gather | bytes 73728 | tf_op jit(solution)/shard_map/all_gather | solution.py:497
  28.8 0.1 multiply_reduce_fusion
  28.9 0.6 fusion.10
  29.5 0.9 fusion.22
  30.4 0.8 convert_reduce_fusion.1
  31.2 19.2 %all-gather.6.cloned.1.call-done = bf16[128,128,128]{2,1,0:T(8,128)(2,1)} async-done(((bf16[16,128,128]{2,1,0:T(8,128)(2,1)}), bf16[128,128,128]{2,1,0:T(8,128)(2,1)}) %all-gather.6.cloned.1.call-update) | async-done | bytes 4194320 | tf_op jit(solution)/shard_map/all_gather | solution.py:496
  50.4 3.1 %fusion = bf16[16,128,128]{2,1,0:T(8,128)(2,1)S(1)} fusion(bf16[8,16,128,128]{3,2,1,0:T(8,128)(2,1)} %bitcast.43, f32[8]{0:T(128)S(1)} %compare_convert_fusion), kind=kLoop, calls=%fused_computation.1 | loop fusion | flops 6029312 | bytes 4718624 | tf_op jit(solution)/shard_map/reduce_sum | solution.py:499
  53.5 0.5 convolution_bitcast_fusion.1
  54.0 0.4 fusion.3
  54.4 95.2 %all-gather.4.cloned.1.call-done = bf16[2048,2048]{1,0:T(8,128)(2,1)} async-done(((bf16[64,2048]{1,0:T(8,128)(2,1)}), bf16[2048,2048]{1,0:T(8,128)(2,1)}) %all-gather.4.cloned.1.call-update) | async-done | bytes 8388624 | tf_op jit(solution)/shard_map/all_gather | solution.py:506
  149.7 4.7 %fusion.5 = (f32[128]{0:T(128)S(1)}, bf16[128,2048]{1,0:T(8,128)(2,1)S(1)}) fusion(bf16[128,2048]{0,1:T(8,128)(2,1)S(1)} %bitcast.46, bf16[2048,2048]{1,0:T(8,128)(2,1)} %all-gather.4.cloned.1.call-done), kind=kOutput, calls=%fused_computation.20 | convolution fusion | flops 1074790272 | bytes 9437696 | tf_op jit(solution)/shard_map/dot_general | solution.py:504
  154.4 1.0 fusion.7.normed
  155.4 115.7 %shard_map.103 = (f32[1,128]{1,0:T(1,128)}, f32[8,128]{1,0:T(8,128)}) custom-call(bf16[128,2048]{1,0:T(8,128)(2,1)} %fusion.7.normed, s32[1,128]{1,0:T(1,128)} %targets.1, s32[32]{0:T(128)} %domains.1, bf16[2048,896]{1,0:T(8,128)(2,1)} %w_hbm.1), custom_call_target="tpu_custom_call" | custom-call | tf_op jit(solution)/shard_map/pallas_call | solution.py:417
  271.1 1.2 slice_bitcast_fusion
  272.3 1.1 copy.51
  (14 shorter events, 0.1 us)
Async XLA Ops:
  7.2 5.3 %copy-start = (bf16[1,128,2048]{2,1,0:T(8,128)(2,1)S(1)}, bf16[1,128,2048]{2,1,0:T(8,128)(2,1)}, u32[]{:S(2)}) copy-start(bf16[1,128,2048]{2,1,0:T(8,128)(2,1)} %param.9) | copy-start | bytes 1572868
  7.2 5.0 %copy-start.2 = (bf16[1,128,2048]{2,1,0:T(8,128)(2,1)S(1)}, bf16[1,128,2048]{2,1,0:T(8,128)(2,1)}, u32[]{:S(2)}) copy-start(bf16[1,128,2048]{2,1,0:T(8,128)(2,1)} %param.8) | copy-start | bytes 1572868
  7.2 43.2 %all-gather.6.cloned.1.call-start = ((), (), s32[]{:S(2)}) async-start(), calls=%async_computation.1 | async-start | bytes 4718592 | tf_op jit(solution)/shard_map/all_gather | solution.py:496
  11.4 138.2 %all-gather.4.cloned.1.call-start = ((), (), s32[]{:S(2)}) async-start(), calls=%async_computation | async-start | bytes 8650752 | tf_op jit(solution)/shard_map/all_gather | solution.py:506
  149.7 4.8 %copy-start.3 = (f32[2048]{0:T(1024)S(1)}, f32[2048]{0:T(1024)}, u32[]{:S(2)}) copy-start(f32[2048]{0:T(1024)} %param.12) | copy-start | bytes 24580
  154.4 119.0 %copy-start.1 = (bf16[128,2048]{1,0:T(8,128)(2,1)}, bf16[128,2048]{1,0:T(8,128)(2,1)S(1)}, u32[]{:S(2)}) copy-start(bf16[128,2048]{1,0:T(8,128)(2,1)S(1)} %get-tuple-element.40) | copy-start | bytes 1572868
Sparse Core Ops, SparseCore 0:
  11.5 38.8 all-gather.5
  53.0 96.6 all-gather.3

commit v3 on v2

--- a/solution.py
+++ b/solution.py
@@ -59,7 +59,7 @@
     )
 
 
-def entry_barrier(here):
+def greet_all(here):
     barrier = pltpu.get_barrier_semaphore()
 
     def greet(i, _):
@@ -68,7 +68,10 @@
         return 0
 
     lax.fori_loop(1, 16, greet, 0)
-    pl.semaphore_wait(barrier, 30)
+
+
+def await_all():
+    pl.semaphore_wait(pltpu.get_barrier_semaphore(), 30)
 
 
 class VocabRing:
@@ -161,22 +164,29 @@
 
 
 class PlaneGather:
-    def __init__(self, here, buf, rows, send, recv):
-        self.here, self.buf, self.height, self.send_sem, self.recv_sem = here, buf, rows, send, recv
+    def __init__(self, here, view, send, recv):
+        self.here, self.view, self.send_sem, self.recv_sem = here, view, send, recv
 
     def copy(self, half, name, at_receiver):
         a, b, part, axis, by = HALF[name]
         if at_receiver:
             a, b = (a - by, b) if axis == "A" else (a, b - by)
         first, second = ("x", "y") if half == 0 else ("y", "x")
-        slot = self.here.slot(a, b) if half == 0 else self.here.slot(b, a)
-        unit = self.height // 4
-        row, count = {"all": (0, 2 * unit), "lo": (0, unit), "hi": (unit, unit)}[part]
-        ref = self.buf.at[slot, pl.ds(half * 2 * unit + row, count)]
+        dx, dy = (a, b) if half == 0 else (b, a)
+        start, count = {"all": (0, 2), "lo": (0, 1), "hi": (1, 1)}[part]
+        column, row = lax.rem(self.here.x + dx + NX, NX), lax.rem(self.here.y + dy + NY, NY)
+        ref = self.view(column, row, half * 2 + start, count)
         n = half * len(ORDER) + ORDER.index(name)
         return remote(
             ref, ref, self.send_sem.at[n], self.recv_sem.at[n], self.here.step(first if axis == "A" else second, by)
         )
+
+    def begin_along(self, axis):
+        half = 0 if axis == "x" else 1
+        for name in ("A1+", "A1-"):
+            self.copy(half, name, False).start()
+        for name in ("B1+o", "B1-o"):
+            self.copy(1 - half, name, False).start()
 
     def send(self, *names):
         for name in names:
@@ -230,7 +240,7 @@
     ((2, 1), (-1, 2)),
     ((1, 2), (2, 2)),
 )
-EVENTS = ((1, 2), (3,), (4,), (), (5,), (6, 7), (), (8,))
+EVENTS = ((), (3,), (4,), (), (5,), (6, 7), (), (8,))
 
 
 def pick(table, i):
@@ -272,7 +282,7 @@
     return jnp.where(lane == 0, peak, jnp.where(lane == 1, total, jnp.where(lane == 2, hit, 0.0)))
 
 
-def vocab_part(here, gather, ring, acts, wv, tg, tcol, out_stats, in_stats, ssend, srecv, tsend, trecv):
+def vocab_part(here, gather, acts, wv, tg, tcol, out_stats, in_stats, ssend, srecv, tsend, trecv):
     def columns(slot):
         wide = jnp.broadcast_to(tg[slot].astype(jnp.float32), (BLOCK, BLOCK))
         tcol[slot] = wide.T
@@ -283,19 +293,17 @@
         columns(slot)
         return 0
 
+    columns(here.pos)
+    lax.fori_loop(1, 16, take_targets, 0)
+
     def batch(i, _):
         for n, events in enumerate(EVENTS):
-            if events or n == 0:
+            if events:
 
                 @pl.when(i == n)
                 def _():
-                    if n == 0:
-                        columns(here.pos)
-                        lax.fori_loop(1, 16, take_targets, 0)
                     for e in events:
                         gather.event(e)
-                    if n == 0:
-                        ring.finish_recv()
 
         slots = []
         for half in (0, 1):
@@ -379,18 +387,215 @@
     lax.fori_loop(1, 16, one, 0)
 
 
-def back_kernel(
-    normed, targets, domains, w_hbm, loss_ref, mean_ref,
-    acts, wv, tg, tcol, out_stats, in_stats, dom,
-    near, gsend, grecv, rsend, rrecv, rpsend, rprecv, tsend, trecv, ssend, srecv, dsend, drecv,
+HALF_HEADS = HEADS // 2
+CHUNKS = 4
+PER = HALF_HEADS // CHUNKS
+
+
+def feature(inputs):
+    wide = inputs.astype(jnp.float32)
+    return jnp.where(wide > 0.0, wide + 1.0, jnp.exp(jnp.minimum(wide, 0.0))).astype(jnp.bfloat16)
+
+
+def head_slice(h):
+    return pl.ds(pl.multiple_of(h * HD, HD), HD)
+
+
+def local_states(keys, values, kf, state, sums):
+    def one(h, _):
+        cols = head_slice(h)
+        feat = feature(keys[:, cols])
+        kf[:, cols] = feat
+        group, n = lax.div(h, HALF_HEADS), lax.rem(h, HALF_HEADS)
+        state[group, n] = lax.dot_general(
+            feat, values[:, cols], (((0,), (0,)), ((), ())), preferred_element_type=jnp.float32
+        )
+        sums[group, n] = jnp.sum(feat.astype(jnp.float32), axis=0, keepdims=True)
+        return 0
+
+    lax.fori_loop(0, HEADS, one, 0)
+
+
+def inner_blocks(queries, kf, values, qf, probs, numer):
+    row = lax.broadcasted_iota(jnp.int32, (BLOCK, BLOCK), 0)
+    causal = row >= lax.broadcasted_iota(jnp.int32, (BLOCK, BLOCK), 1)
+
+    def one(h, _):
+        cols = head_slice(h)
+        feat = feature(queries[:, cols])
+        qf[:, cols] = feat
+        scores = lax.dot_general(feat, kf[:, cols], (((1,), (1,)), ((), ())), preferred_element_type=jnp.float32)
+        prob = jnp.where(causal, scores, 0.0).astype(jnp.bfloat16)
+        probs[h] = prob
+        numer[:, cols] = jnp.dot(prob, values[:, cols], preferred_element_type=jnp.float32)
+        return 0
+
+    lax.fori_loop(0, HEADS, one, 0)
+
+
+def outer_blocks(first, qf, probs, numer, state_in, sum_in, out):
+    def one(n, _):
+        h = first + n
+        cols = head_slice(h)
+        group, n = lax.div(h, HALF_HEADS), lax.rem(h, HALF_HEADS)
+        feat = qf[:, cols]
+        top = numer[:, cols] + jnp.dot(feat, state_in[group, n], preferred_element_type=jnp.float32)
+        below = probs[h].astype(jnp.float32) + feat.astype(jnp.float32) * sum_in[group, n]
+        out[:, cols] = (top / jnp.sum(below, axis=1, keepdims=True)).astype(jnp.bfloat16)
+        return 0
+
+    lax.fori_loop(0, HALF_HEADS, one, 0)
+
+
+class Prefix:
+    def __init__(self, here, refs, sems):
+        self.here = here
+        (self.state, self.sums, self.part, self.ksum, self.cin, self.kin, self.cout, self.kout,
+         self.stage, self.kstage, self.state_in, self.sum_in) = refs
+        (self.xsend, self.xrecv, self.csend, self.crecv, self.fsend, self.frecv) = sems
+        self.partner = here.at(c=1 - here.c)
+        self.up = here.step("y", 1)
+
+    def exchange(self):
+        other = 1 - self.here.c
+        return (
+            remote(self.state.at[other], self.part, self.xsend.at[0], self.xrecv.at[0], self.partner),
+            remote(self.sums.at[other], self.ksum, self.xsend.at[1], self.xrecv.at[1], self.partner),
+        )
+
+    def climb(self, j):
+        heads = pl.ds(j * PER, PER)
+        copies = [remote(self.cout.at[heads], self.cin.at[heads], self.csend.at[j], self.crecv.at[j], self.up)]
+        if j == 0:
+            copies.append(remote(self.kout, self.kin, self.csend.at[CHUNKS], self.crecv.at[CHUNKS], self.up))
+        return copies
+
+    def give(self, j):
+        heads = pl.ds(j * PER, PER)
+        there = self.state_in.at[self.here.c, heads]
+        copies = [remote(self.stage.at[heads], there, self.fsend.at[j], self.frecv.at[j], self.partner)]
+        if j == 0:
+            copies.append(
+                remote(self.kstage, self.sum_in.at[self.here.c], self.fsend.at[CHUNKS], self.frecv.at[CHUNKS], self.partner)
+            )
+        return copies
+
+    def chunk(self, j):
+        here = self.here
+
+        @pl.when(here.y > 0)
+        def _():
+            for copy in self.climb(j):
+                copy.wait_recv()
+
+        second = (here.c == 1).astype(jnp.float32)
+        heads = pl.ds(j * PER, PER)
+        before = self.cin[heads].astype(jnp.float32)
+        own, other = self.state[here.c, heads], self.part[heads]
+        self.cout[heads] = (before + (own + other)).astype(jnp.bfloat16)
+        if j == 0:
+            kbefore, kown, kother = self.kin[...], self.sums[here.c], self.ksum[...]
+            self.kout[...] = kbefore + (kown + kother)
+
+        @pl.when(here.y < NY - 1)
+        def _():
+            for copy in self.climb(j):
+                copy.start()
+
+        self.stage[heads] = (before + own * (1.0 - second)).astype(jnp.bfloat16)
+        self.state_in[here.c, heads] = (before + other * second).astype(jnp.bfloat16)
+        if j == 0:
+            self.kstage[...] = kbefore + kown * (1.0 - second)
+            self.sum_in[here.c] = kbefore + kother * second
+        for copy in self.give(j):
+            copy.start()
+
+    def take(self):
+        for j in range(CHUNKS):
+            heads = pl.ds(j * PER, PER)
+            other = 1 - self.here.c
+            remote(
+                self.stage.at[heads], self.state_in.at[other, heads], self.fsend.at[j], self.frecv.at[j], self.partner
+            ).wait_recv()
+        remote(
+            self.kstage, self.sum_in.at[other], self.fsend.at[CHUNKS], self.frecv.at[CHUNKS], self.partner
+        ).wait_recv()
+
+    def finish_send(self):
+        for copy in self.exchange():
+            copy.wait_send()
+        for j in range(CHUNKS):
+            for copy in self.give(j):
+                copy.wait_send()
+
+            @pl.when(self.here.y < NY - 1)
+            def _():
+                for copy in self.climb(j):
+                    copy.wait_send()
+
+
+def normalise(projected, gain, out):
+    def rows(r, _):
+        some = pl.ds(pl.multiple_of(r * 16, 16), 16)
+        wide = projected[some].astype(jnp.float32)
+        scale = lax.rsqrt(jnp.mean(wide * wide, axis=1, keepdims=True) + 1e-05)
+        out[some] = (wide * scale * gain[...]).astype(jnp.bfloat16)
+        return 0
+
+    lax.fori_loop(0, BLOCK // 16, rows, 0)
+
+
+def whole_kernel(
+    queries, keys, values, gain, targets, domains, wo_hbm, w_hbm, projected, loss_ref, mean_ref,
+    qf, kf, probs, numer, state, sums, part, ksum, cin, kin, cout, kout, stage, kstage, state_in, sum_in,
+    attended, wo, halves, given, acts, wv, tg, tcol, out_stats, in_stats, dom,
+    near, xsend, xrecv, csend, crecv, fsend, frecv, zsend, zrecv, hsend, hrecv, psend, precv,
+    gsend, grecv, rsend, rrecv, rpsend, rprecv, tsend, trecv, ssend, srecv, dsend, drecv,
 ):
     here = Place()
-    acts[here.pos] = normed[...]
+    cin[...] = jnp.zeros_like(cin)
+    kin[...] = jnp.zeros_like(kin)
+    greet_all(here)
+    partner = here.at(c=1 - here.c)
+    half = D // 2
+    wo_rows = pl.ds(pl.multiple_of(here.y * 16, 16), 16)
+    wo_own = wo_hbm.at[wo_rows, pl.ds(pl.multiple_of(here.c * half, half), half)]
+    wo_place = wo.at[here.x, here.z, here.y]
+    own_wo = pltpu.make_async_copy(wo_own, wo_place, near.at[1])
+    own_wo.start()
     tg[here.pos] = targets[...]
-    entry_barrier(here)
-    ring = VocabRing(here, w_hbm, wv, near, rsend, rrecv, rpsend, rprecv)
-    gather = PlaneGather(here, acts, BLOCK, gsend, grecv)
-    gather.begin()
+    local_states(keys, values, kf, state, sums)
+    await_all()
+
+    def wo_peer(i):
+        z = lax.rem(here.z + i, NZ)
+        return z, here.at(z=z)
+
+    def wo_give(i, _):
+        z, to = wo_peer(i)
+        remote(wo_own, wo_place, zsend.at[i], zrecv.at[here.z], to).start()
+        return 0
+
+    def wo_take(i, _):
+        z, to = wo_peer(i)
+        place = wo.at[here.x, z, here.y]
+        remote(place, place, zsend.at[i], zrecv.at[z], to).wait_recv()
+        return 0
+
+    def wo_sent(i, _):
+        z, to = wo_peer(i)
+        remote(wo_own, wo_place, zsend.at[i], zrecv.at[here.z], to).wait_send()
+        return 0
+
+    lax.fori_loop(1, NZ, wo_give, 0)
+    prefix = Prefix(
+        here,
+        (state, sums, part, ksum, cin, kin, cout, kout, stage, kstage, state_in, sum_in),
+        (xsend, xrecv, csend, crecv, fsend, frecv),
+    )
+    for copy in prefix.exchange():
+        copy.start()
+    ring = VocabRing(here, w_hbm, wv, near.at[0], rsend, rrecv, rpsend, rprecv)
     ring.begin()
 
     def give_targets(i, _):
@@ -400,34 +605,142 @@
         return 0
 
     lax.fori_loop(1, 16, give_targets, 0)
-    for k in range(1, 5):
-        ring.advance(k)
-    vocab_part(here, gather, ring, acts, wv, tg, tcol, out_stats, in_stats, ssend, srecv, tsend, trecv)
+    for copy in prefix.exchange():
+        copy.wait_recv()
+
+    @pl.when(here.y == 0)
+    def _():
+        for j in range(CHUNKS):
+            prefix.chunk(j)
+
+    inner_blocks(queries, kf, values, qf, probs, numer)
+    own_wo.wait()
+    lax.fori_loop(1, NZ, wo_take, 0)
+    weights = PlaneGather(here, lambda x, y, start, count: wo.at[x, pl.ds(start * 2, count * 2), y], psend, precv)
+    weights.begin_along("x")
+
+    @pl.when(here.y > 0)
+    def _():
+        for j in range(CHUNKS):
+            prefix.chunk(j)
+
+    weights.begin_along("y")
+    weights.event(1)
+    prefix.take()
+    mine = attended.at[here.c]
+    outer_blocks(0, qf, probs, numer, state_in, sum_in, mine)
+    weights.event(2)
+    weights.event(3)
+    outer_blocks(HALF_HEADS, qf, probs, numer, state_in, sum_in, mine)
+    rows_over = remote(mine, mine, hsend.at[0], hrecv.at[0], partner)
+    rows_over.start()
+    ring.advance(1)
+    weights.event(4)
+    weights.event(5)
+    weights.event(6)
+    weights.event(7)
+    theirs = attended.at[1 - here.c]
+    remote(theirs, theirs, hsend.at[0], hrecv.at[0], partner).wait_recv()
+    weights.event(8)
+
+    def project(n, _):
+        cols = pl.ds(pl.multiple_of(n * TILE, TILE), TILE)
+        rows = jnp.concatenate([attended[0], attended[1]], axis=0)
+        w = wo[:, :, :, :, cols].reshape(D, TILE)
+        both = jnp.dot(rows, w, preferred_element_type=jnp.float32).astype(jnp.bfloat16)
+        low = here.c == 0
+        halves[here.c, :, cols] = jnp.where(low, both[:BLOCK], both[BLOCK:])
+        given[:, cols] = jnp.where(low, both[BLOCK:], both[:BLOCK])
+        return 0
+
+    lax.fori_loop(0, half // TILE, project, 0)
+    back = remote(given, halves.at[here.c], hsend.at[1], hrecv.at[1], partner)
+    back.start()
+    other = halves.at[1 - here.c]
+    remote(given, other, hsend.at[1], hrecv.at[1], partner).wait_recv()
+    projected[:, :half] = halves[0]
+    projected[:, half:] = halves[1]
+    normalise(projected, gain, acts.at[here.pos])
+    unit = BLOCK // 4
+    gather = PlaneGather(
+        here, lambda x, y, start, count: acts.at[x * NY + y, pl.ds(start * unit, count * unit)], gsend, grecv
+    )
+    gather.begin()
+    ring.advance(2)
+    gather.event(1)
+    gather.event(2)
+    ring.advance(3)
+    ring.advance(4)
+    ring.finish_recv()
+    vocab_part(here, gather, acts, wv, tg, tcol, out_stats, in_stats, ssend, srecv, tsend, trecv)
     losses = losses_of(here, out_stats, in_stats, ssend, srecv)
     loss_ref[...] = losses
     mean_ref[...] = domain_part(here, losses, domains, dom, dsend, drecv)
+    lax.fori_loop(1, NZ, wo_sent, 0)
+    prefix.finish_send()
+    weights.finish_send()
+    rows_over.wait_send()
+    back.wait_send()
     gather.finish_send()
     ring.finish_send()
     finish_sends(here, out_stats, in_stats, ssend, srecv, tg, tsend, trecv, dom, dsend, drecv)
 
 
-def back(normed, targets, domains, w_vocab):
+def on_device(queries, keys, values, w_out, norm_gain, w_vocab, targets, domains):
     vmem = pl.BlockSpec(memory_space=pltpu.VMEM)
     dma = pltpu.SemaphoreType.DMA
-    return pl.pallas_call(
-        back_kernel,
-        out_shape=(jax.ShapeDtypeStruct((1, BLOCK), jnp.float32), jax.ShapeDtypeStruct((8, 128), jnp.float32)),
-        in_specs=[vmem, vmem, pl.BlockSpec(memory_space=pltpu.SMEM), pl.BlockSpec(memory_space=pl.ANY)],
-        out_specs=(vmem, vmem),
+    low, wide = jnp.bfloat16, jnp.float32
+    projected, losses, means = pl.pallas_call(
+        whole_kernel,
+        out_shape=(
+            jax.ShapeDtypeStruct((BLOCK, D), low),
+            jax.ShapeDtypeStruct((1, BLOCK), wide),
+            jax.ShapeDtypeStruct((8, 128), wide),
+        ),
+        in_specs=[vmem] * 5
+        + [pl.BlockSpec(memory_space=pltpu.SMEM), pl.BlockSpec(memory_space=pl.ANY), pl.BlockSpec(memory_space=pl.ANY)],
+        out_specs=(vmem, vmem, vmem),
         scratch_shapes=[
-            pltpu.VMEM((16, BLOCK, D), jnp.bfloat16),
-            pltpu.VMEM((NZ, D, TILE), jnp.bfloat16),
+            pltpu.VMEM((BLOCK, D), low),
+            pltpu.VMEM((BLOCK, D), low),
+            pltpu.VMEM((HEADS, BLOCK, BLOCK), low),
+            pltpu.VMEM((BLOCK, D), wide),
+            pltpu.VMEM((2, HALF_HEADS, HD, HD), wide),
+            pltpu.VMEM((2, HALF_HEADS, 1, HD), wide),
+            pltpu.VMEM((HALF_HEADS, HD, HD), wide),
+            pltpu.VMEM((HALF_HEADS, 1, HD), wide),
+            pltpu.VMEM((HALF_HEADS, HD, HD), low),
+            pltpu.VMEM((HALF_HEADS, 1, HD), wide),
+            pltpu.VMEM((HALF_HEADS, HD, HD), low),
+            pltpu.VMEM((HALF_HEADS, 1, HD), wide),
+            pltpu.VMEM((HALF_HEADS, HD, HD), low),
+            pltpu.VMEM((HALF_HEADS, 1, HD), wide),
+            pltpu.VMEM((2, HALF_HEADS, HD, HD), low),
+            pltpu.VMEM((2, HALF_HEADS, 1, HD), wide),
+            pltpu.VMEM((2, BLOCK, D), low),
+            pltpu.VMEM((NX, NZ, NY, 16, D // 2), low),
+            pltpu.VMEM((2, BLOCK, D // 2), low),
+            pltpu.VMEM((BLOCK, D // 2), low),
+            pltpu.VMEM((16, BLOCK, D), low),
+            pltpu.VMEM((NZ, D, TILE), low),
             pltpu.VMEM((16, 1, BLOCK), jnp.int32),
-            pltpu.VMEM((16, BLOCK, BLOCK), jnp.float32),
-            pltpu.VMEM((16, 8, 128), jnp.float32),
-            pltpu.VMEM((16, 8, 128), jnp.float32),
-            pltpu.VMEM((2, 16, 8, 128), jnp.float32),
-            dma(()),
+            pltpu.VMEM((16, BLOCK, BLOCK), wide),
+            pltpu.VMEM((16, 8, 128), wide),
+            pltpu.VMEM((16, 8, 128), wide),
+            pltpu.VMEM((2, 16, 8, 128), wide),
+            dma((2,)),
+            dma((2,)),
+            dma((2,)),
+            dma((CHUNKS + 1,)),
+            dma((CHUNKS + 1,)),
+            dma((CHUNKS + 1,)),
+            dma((CHUNKS + 1,)),
+            dma((NZ,)),
+            dma((NZ,)),
+            dma((2,)),
+            dma((2,)),
+            dma((40,)),
+            dma((40,)),
             dma((40,)),
             dma((40,)),
             dma((2, 4)),
@@ -444,74 +757,8 @@
         compiler_params=pltpu.CompilerParams(
             collective_id=0, has_side_effects=True, vmem_limit_bytes=60 * 1024 * 1024
         ),
-    )(normed, targets, domains, w_vocab)
-
-
-def features(inputs):
-    return (1.0 + jax.nn.elu(inputs.astype(jnp.float32))).astype(jnp.bfloat16)
-
-
-def attend_blocks(query_feat, key_feat, value_blk, block_states, block_keys, state_in, sum_in):
-    causal = jnp.tril(jnp.ones((BLOCK, BLOCK), dtype=bool))
-
-    def block_step(carry, inputs):
-        state, key_sum = carry
-        blk_query, blk_key, blk_value, blk_state, blk_keysum = inputs
-        scores = jnp.einsum("thf,shf->hts", blk_query, blk_key, preferred_element_type=jnp.float32)
-        probs = jnp.where(causal[None], scores, 0.0).astype(jnp.bfloat16)
-        numer = jnp.einsum("hts,she->the", probs, blk_value, preferred_element_type=jnp.float32)
-        numer = numer + jnp.einsum(
-            "thf,hfe->the",
-            blk_query,
-            state.astype(jnp.bfloat16),
-            preferred_element_type=jnp.float32,
-        )
-        denom = jnp.sum(probs, axis=2, dtype=jnp.float32).T
-        denom = denom + jnp.einsum(
-            "thf,hf->th", blk_query.astype(jnp.float32), key_sum, precision=lax.Precision.HIGHEST
-        )
-        outputs = (numer / denom[:, :, None]).astype(jnp.bfloat16)
-        return ((state + blk_state, key_sum + blk_keysum), outputs)
-
-    _, outputs = lax.scan(
-        block_step, (state_in, sum_in), (query_feat, key_feat, value_blk, block_states, block_keys)
-    )
-    return outputs
-
-
-def on_device(queries, keys, values, w_out, norm_gain, w_vocab, targets, domains):
-    tokens = queries.shape[1]
-    blocks = tokens // BLOCK
-    width = HEADS * HD
-    query_feat = features(queries[0]).reshape(blocks, BLOCK, HEADS, HD)
-    key_feat = features(keys[0]).reshape(blocks, BLOCK, HEADS, HD)
-    value_blk = values[0].reshape(blocks, BLOCK, HEADS, HD)
-    block_states = jnp.einsum(
-        "bshf,bshe->bhfe", key_feat, value_blk, preferred_element_type=jnp.float32
-    )
-    block_keys = jnp.sum(key_feat, axis=1, dtype=jnp.float32)
-    state_local = jnp.sum(block_states, axis=0)
-    sum_local = jnp.sum(block_keys, axis=0)
-    seq_count, seq_mine = (lax.axis_size("seq"), lax.axis_index("seq"))
-    pieces = lax.all_gather(state_local.astype(jnp.bfloat16), "seq")
-    sums = lax.all_gather(sum_local, "seq")
-    earlier = (jnp.arange(seq_count) < seq_mine).astype(jnp.float32)
-    state_in = jnp.sum(pieces.astype(jnp.float32) * earlier[:, None, None, None], axis=0)
-    sum_in = jnp.sum(sums * earlier[:, None, None], axis=0)
-    attended = attend_blocks(
-        query_feat, key_feat, value_blk, block_states, block_keys, state_in, sum_in
-    ).reshape(tokens, width)
-    projected = jnp.dot(
-        attended,
-        lax.all_gather(w_out, "doc", axis=0, tiled=True),
-        preferred_element_type=jnp.float32,
-    ).astype(jnp.bfloat16)
-    wide = projected.astype(jnp.float32)
-    normed = (
-        wide * lax.rsqrt(jnp.mean(wide * wide, axis=-1, keepdims=True) + 1e-05) * norm_gain
-    ).astype(jnp.bfloat16)
-    own_losses, means = back(normed, targets, domains, w_vocab)
-    return (projected[None], own_losses, means[0, :DOMAINS])
+    )(queries[0], keys[0], values[0], norm_gain[None], targets, domains, w_out, w_vocab)
+    return (projected[None], losses, means[0, :DOMAINS])
 
 
 def solution(mesh):

time: 281 us -> 143 us (0.51)
  waiting for transfers between devices: 115 us -> 0 us
  Pallas kernels: 116 us -> 138 us
  blocking collectives: 15.8 us -> 0 us
  between operations: 14.2 us -> 0.64 us
  matrix products: 8.92 us -> 0 us
  other arithmetic: 6.59 us -> 0 us
    all_gather x2 -> x0, waiting for transfers between devices: 114 us -> none  [the longest x1 95.2 us: on_device(): lax.all_gather(w_out, 'doc', axis=0, tiled=True)]
    pallas_call x1, Pallas kernels: 116 us -> 138 us  [on_device(): pl.pallas_call(whole_kernel, out_shape=(jax.ShapeDtypeStruct((BLOCK, D),...]
    all_gather x1 -> x0, blocking collectives: 15.8 us -> none  [on_device(): sums = lax.all_gather(sum_local, 'seq')]
    dot_general x6 -> x0, matrix products: 8.92 us -> none  [the longest x1 4.75 us: on_device(): jnp.dot(attended, lax.all_gather(w_out, 'doc', axis=0, tiled=True), prefe...]
    reduce_sum x3 -> x0, other arithmetic: 3.69 us -> none  [the longest x1 3.13 us: on_device(): jnp.sum(pieces.astype(jnp.float32) * earlier[:, None, None, None], axis=0)]
  transfers between devices with their start and end apart: 2 -> 0, of which waited for: 2 -> 0; matrix products, arithmetic and copies ran while one was open for 3% -> 0% of each run, Pallas kernels for 0% -> 0%
where the time goes in v3:
time: 143 us; the launch traced here: 142 us
  Pallas kernels  138 us (97%)
  local copies, waits for them, and re-layouts  4.25 us (3%)
    pallas_call x1, Pallas kernels, on_device(): pl.pallas_call(whole_kernel, out_shape=(jax.ShapeDtypeStruct((BLOCK, D),...  138 us
    unnamed x2, local copies, waits for them, and re-layouts  3.06 us

profile of v3, /device:TPU:1, one launch (start us, length us, event | category | flops | bytes accessed | tf_op | source)
XLA Modules:
  0.0 142.5 jit_solution(12526652904011384334)
XLA Ops:
  0.6 137.6 %shard_map.103 = (bf16[128,2048]{1,0:T(8,128)(2,1)}, f32[1,128]{1,0:T(1,128)}, f32[8,128]{1,0:T(8,128)}) custom-call(bf16[128,2048]{1,0:T(8,128)(2,1)} %bitcast.7, bf16[128,2048]{1,0:T(8,128)(2,1)} %bitcast.8, bf16[128,2048]{1,0:T(8,128)(2,1)} %bitcast.9, f32[1,2048]{1,0:T(1,128)} %bitcast.11, s32[1,128]{1,0:T(1,128)} %targets.1, s32[32]{0:T(128)} %domains.1, ...), custom_call_target="tpu_custom_call" | custom-call | tf_op jit(solution)/shard_map/pallas_call | solution.py:693
  138.2 1.2 slice_bitcast_fusion
  139.4 1.9 %copy.13 = bf16[1,128,2048]{2,1,0:T(8,128)(2,1)} copy(bf16[1,128,2048]{2,1,0:T(8,128)(2,1)} %bitcast.10) | data formatting | bytes 1048576
  141.3 1.2 copy.14

commit v4 on v3

--- a/solution.py
+++ b/solution.py
@@ -161,11 +161,13 @@
     "B2-h": (2, 1, "hi", "B", -1),
 }
 ORDER = list(HALF)
+WO_CUTS = ((0, 1, 3), (3, 5, 8))
+ROW_CUTS = ((0, 32, 64), (64, 96, 128))
 
 
 class PlaneGather:
-    def __init__(self, here, view, send, recv):
-        self.here, self.view, self.send_sem, self.recv_sem = here, view, send, recv
+    def __init__(self, here, view, cuts, send, recv):
+        self.here, self.view, self.cuts, self.send_sem, self.recv_sem = here, view, cuts, send, recv
 
     def copy(self, half, name, at_receiver):
         a, b, part, axis, by = HALF[name]
@@ -173,9 +175,10 @@
             a, b = (a - by, b) if axis == "A" else (a, b - by)
         first, second = ("x", "y") if half == 0 else ("y", "x")
         dx, dy = (a, b) if half == 0 else (b, a)
-        start, count = {"all": (0, 2), "lo": (0, 1), "hi": (1, 1)}[part]
+        first_row, middle, last_row = self.cuts[half]
+        start, stop = {"all": (first_row, last_row), "lo": (first_row, middle), "hi": (middle, last_row)}[part]
         column, row = lax.rem(self.here.x + dx + NX, NX), lax.rem(self.here.y + dy + NY, NY)
-        ref = self.view(column, row, half * 2 + start, count)
+        ref = self.view(column, row, start, stop - start)
         n = half * len(ORDER) + ORDER.index(name)
         return remote(
             ref, ref, self.send_sem.at[n], self.recv_sem.at[n], self.here.step(first if axis == "A" else second, by)
@@ -188,41 +191,41 @@
         for name in ("B1+o", "B1-o"):
             self.copy(1 - half, name, False).start()
 
-    def send(self, *names):
+    def send(self, halves, *names):
         for name in names:
-            for half in (0, 1):
+            for half in halves:
                 self.copy(half, name, False).start()
 
-    def take(self, *names):
+    def take(self, halves, *names):
         for name in names:
-            for half in (0, 1):
+            for half in halves:
                 self.copy(half, name, True).wait_recv()
 
     def begin(self):
-        self.send("A1+", "A1-", "B1+o", "B1-o")
-
-    def event(self, e):
+        self.send((0, 1), "A1+", "A1-", "B1+o", "B1-o")
+
+    def event(self, e, halves=(0, 1)):
         if e == 1:
-            self.take("A1+", "A1-")
-            self.send("A2+", "A2-", "B1+m", "B1-m", "B1+p", "B1-p")
+            self.take(halves, "A1+", "A1-")
+            self.send(halves, "A2+", "A2-", "B1+m", "B1-m", "B1+p", "B1-p")
         elif e == 2:
-            self.take("B1+o", "B1-o")
-            self.send("B2+o", "B2-o")
+            self.take(halves, "B1+o", "B1-o")
+            self.send(halves, "B2+o", "B2-o")
         elif e == 3:
-            self.take("A2+", "A2-")
-            self.send("B1+l", "B1-l", "B1+h", "B1-h")
+            self.take(halves, "A2+", "A2-")
+            self.send(halves, "B1+l", "B1-l", "B1+h", "B1-h")
         elif e == 4:
-            self.take("B1+p", "B1-p", "B1+m", "B1-m")
-            self.send("B2+p", "B2-m")
+            self.take(halves, "B1+p", "B1-p", "B1+m", "B1-m")
+            self.send(halves, "B2+p", "B2-m")
         elif e == 5:
-            self.take("B2+o", "B2-o")
+            self.take(halves, "B2+o", "B2-o")
         elif e == 6:
-            self.take("B1+l", "B1-l", "B1+h", "B1-h")
-            self.send("B2+l", "B2-h")
+            self.take(halves, "B1+l", "B1-l", "B1+h", "B1-h")
+            self.send(halves, "B2+l", "B2-h")
         elif e == 7:
-            self.take("B2+p", "B2-m")
+            self.take(halves, "B2+p", "B2-m")
         else:
-            self.take("B2+l", "B2-h")
+            self.take(halves, "B2+l", "B2-h")
 
     def finish_send(self):
         for name in ORDER:
@@ -282,7 +285,7 @@
     return jnp.where(lane == 0, peak, jnp.where(lane == 1, total, jnp.where(lane == 2, hit, 0.0)))
 
 
-def vocab_part(here, gather, acts, wv, tg, tcol, out_stats, in_stats, ssend, srecv, tsend, trecv):
+def target_columns(here, tg, tcol, tsend, trecv):
     def columns(slot):
         wide = jnp.broadcast_to(tg[slot].astype(jnp.float32), (BLOCK, BLOCK))
         tcol[slot] = wide.T
@@ -296,6 +299,8 @@
     columns(here.pos)
     lax.fori_loop(1, 16, take_targets, 0)
 
+
+def vocab_part(here, gather, acts, wv, tcol, out_stats, in_stats, ssend, srecv):
     def batch(i, _):
         for n, events in enumerate(EVENTS):
             if events:
@@ -416,11 +421,12 @@
     lax.fori_loop(0, HEADS, one, 0)
 
 
-def inner_blocks(queries, kf, values, qf, probs, numer):
+def inner_blocks(first, queries, kf, values, qf, probs, numer):
     row = lax.broadcasted_iota(jnp.int32, (BLOCK, BLOCK), 0)
     causal = row >= lax.broadcasted_iota(jnp.int32, (BLOCK, BLOCK), 1)
 
-    def one(h, _):
+    def one(n, _):
+        h = first + n
         cols = head_slice(h)
         feat = feature(queries[:, cols])
         qf[:, cols] = feat
@@ -430,7 +436,7 @@
         numer[:, cols] = jnp.dot(prob, values[:, cols], preferred_element_type=jnp.float32)
         return 0
 
-    lax.fori_loop(0, HEADS, one, 0)
+    lax.fori_loop(0, HALF_HEADS, one, 0)
 
 
 def outer_blocks(first, qf, probs, numer, state_in, sum_in, out):
@@ -450,11 +456,10 @@
 class Prefix:
     def __init__(self, here, refs, sems):
         self.here = here
-        (self.state, self.sums, self.part, self.ksum, self.cin, self.kin, self.cout, self.kout,
+        (self.state, self.sums, self.part, self.ksum, self.below, self.kbelow, self.above, self.kabove, self.cout, self.kout,
          self.stage, self.kstage, self.state_in, self.sum_in) = refs
-        (self.xsend, self.xrecv, self.csend, self.crecv, self.fsend, self.frecv) = sems
+        (self.xsend, self.xrecv, self.usend, self.urecv, self.dsend, self.drecv, self.fsend, self.frecv) = sems
         self.partner = here.at(c=1 - here.c)
-        self.up = here.step("y", 1)
 
     def exchange(self):
         other = 1 - self.here.c
@@ -463,15 +468,68 @@
             remote(self.sums.at[other], self.ksum, self.xsend.at[1], self.xrecv.at[1], self.partner),
         )
 
-    def climb(self, j):
-        heads = pl.ds(j * PER, PER)
-        copies = [remote(self.cout.at[heads], self.cin.at[heads], self.csend.at[j], self.crecv.at[j], self.up)]
+    def heads(self, j):
+        return pl.ds(j * PER, PER)
+
+    def move(self, j, src, ksrc, dst, kdst, send, recv, to):
+        heads = self.heads(j)
+        copies = [remote(src.at[heads], dst.at[heads], send.at[j], recv.at[j], to)]
         if j == 0:
-            copies.append(remote(self.kout, self.kin, self.csend.at[CHUNKS], self.crecv.at[CHUNKS], self.up))
+            copies.append(remote(ksrc, kdst, send.at[CHUNKS], recv.at[CHUNKS], to))
         return copies
 
+    def up(self, j):
+        return self.move(
+            j, self.cout, self.kout, self.below, self.kbelow, self.usend, self.urecv, self.here.step("y", 1)
+        )
+
+    def down(self, j, relay):
+        src, ksrc = (self.above, self.kabove) if relay else (self.cout, self.kout)
+        return self.move(j, src, ksrc, self.above, self.kabove, self.dsend, self.drecv, self.here.step("y", -1))
+
+    def total(self, j, add):
+        heads = self.heads(j)
+        value = self.state[self.here.c, heads] + self.part[heads]
+        if add:
+            value = value + self.below[heads].astype(jnp.float32)
+        self.cout[heads] = value.astype(jnp.bfloat16)
+        if j == 0:
+            value = self.sums[self.here.c] + self.ksum[...]
+            self.kout[...] = value + self.kbelow[...] if add else value
+
+    def start(self):
+        @pl.when(self.here.y < 2)
+        def _():
+            for j in range(CHUNKS):
+                self.total(j, False)
+                for copy in self.up(j):
+                    copy.start()
+
+                @pl.when(self.here.y == 0)
+                def _():
+                    for copy in self.down(j, False):
+                        copy.start()
+
+    def relay(self):
+        @pl.when(self.here.y == 2)
+        def _():
+            for j in range(CHUNKS):
+                for copy in self.up(j):
+                    copy.wait_recv()
+                self.total(j, True)
+                for copy in self.up(j):
+                    copy.start()
+
+        @pl.when(self.here.y == 3)
+        def _():
+            for j in range(CHUNKS):
+                for copy in self.down(j, False):
+                    copy.wait_recv()
+                for copy in self.down(j, True):
+                    copy.start()
+
     def give(self, j):
-        heads = pl.ds(j * PER, PER)
+        heads = self.heads(j)
         there = self.state_in.at[self.here.c, heads]
         copies = [remote(self.stage.at[heads], there, self.fsend.at[j], self.frecv.at[j], self.partner)]
         if j == 0:
@@ -480,40 +538,37 @@
             )
         return copies
 
-    def chunk(self, j):
+    def finish(self):
         here = self.here
-
-        @pl.when(here.y > 0)
-        def _():
-            for copy in self.climb(j):
-                copy.wait_recv()
-
         second = (here.c == 1).astype(jnp.float32)
-        heads = pl.ds(j * PER, PER)
-        before = self.cin[heads].astype(jnp.float32)
-        own, other = self.state[here.c, heads], self.part[heads]
-        self.cout[heads] = (before + (own + other)).astype(jnp.bfloat16)
-        if j == 0:
-            kbefore, kown, kother = self.kin[...], self.sums[here.c], self.ksum[...]
-            self.kout[...] = kbefore + (kown + kother)
-
-        @pl.when(here.y < NY - 1)
-        def _():
-            for copy in self.climb(j):
+        for j in range(CHUNKS):
+
+            @pl.when(jnp.logical_or(here.y == 1, here.y == 3))
+            def _():
+                for copy in self.up(j):
+                    copy.wait_recv()
+
+            @pl.when(here.y == 2)
+            def _():
+                for copy in self.down(j, False):
+                    copy.wait_recv()
+
+            heads = self.heads(j)
+            before = self.below[heads].astype(jnp.float32) + self.above[heads].astype(jnp.float32)
+            own, other = self.state[here.c, heads], self.part[heads]
+            self.stage[heads] = (before + own * (1.0 - second)).astype(jnp.bfloat16)
+            self.state_in[here.c, heads] = (before + other * second).astype(jnp.bfloat16)
+            if j == 0:
+                kbefore = self.kbelow[...] + self.kabove[...]
+                self.kstage[...] = kbefore + self.sums[here.c] * (1.0 - second)
+                self.sum_in[here.c] = kbefore + self.ksum[...] * second
+            for copy in self.give(j):
                 copy.start()
 
-        self.stage[heads] = (before + own * (1.0 - second)).astype(jnp.bfloat16)
-        self.state_in[here.c, heads] = (before + other * second).astype(jnp.bfloat16)
-        if j == 0:
-            self.kstage[...] = kbefore + kown * (1.0 - second)
-            self.sum_in[here.c] = kbefore + kother * second
-        for copy in self.give(j):
-            copy.start()
-
     def take(self):
+        other = 1 - self.here.c
         for j in range(CHUNKS):
-            heads = pl.ds(j * PER, PER)
-            other = 1 - self.here.c
+            heads = self.heads(j)
             remote(
                 self.stage.at[heads], self.state_in.at[other, heads], self.fsend.at[j], self.frecv.at[j], self.partner
             ).wait_recv()
@@ -530,7 +585,12 @@
 
             @pl.when(self.here.y < NY - 1)
             def _():
-                for copy in self.climb(j):
+                for copy in self.up(j):
+                    copy.wait_send()
+
+            @pl.when(jnp.logical_or(self.here.y == 0, self.here.y == 3))
+            def _():
+                for copy in self.down(j, False):
                     copy.wait_send()
 
 
@@ -546,16 +606,20 @@
 
 
 def whole_kernel(
-    queries, keys, values, gain, targets, domains, wo_hbm, w_hbm, projected, loss_ref, mean_ref,
-    qf, kf, probs, numer, state, sums, part, ksum, cin, kin, cout, kout, stage, kstage, state_in, sum_in,
-    attended, wo, halves, given, acts, wv, tg, tcol, out_stats, in_stats, dom,
-    near, xsend, xrecv, csend, crecv, fsend, frecv, zsend, zrecv, hsend, hrecv, psend, precv,
+    q_hbm, k_hbm, v_hbm, gain_hbm, targets, domains, wo_hbm, w_hbm, projected, small,
+    queries, keys, values, gain, qf, kf, probs, numer, state, sums, part, ksum, below, kbelow, above, kabove, cout, kout,
+    stage, kstage, state_in, sum_in, attended, wo, halves, given, acts, wv, tg, tcol, out_stats, in_stats, dom,
+    near, xsend, xrecv, usend, urecv, downsend, downrecv, fsend, frecv, zsend, zrecv, hsend, hrecv, psend, precv,
     gsend, grecv, rsend, rrecv, rpsend, rprecv, tsend, trecv, ssend, srecv, dsend, drecv,
 ):
     here = Place()
-    cin[...] = jnp.zeros_like(cin)
-    kin[...] = jnp.zeros_like(kin)
+    for ref in (below, kbelow, above, kabove):
+        ref[...] = jnp.zeros_like(ref)
     greet_all(here)
+    moves = ((k_hbm, keys), (v_hbm, values), (q_hbm, queries), (gain_hbm, gain), (targets, tg.at[here.pos]))
+    loads = [pltpu.make_async_copy(src, dst, near.at[2 + n]) for n, (src, dst) in enumerate(moves)]
+    for load in loads:
+        load.start()
     partner = here.at(c=1 - here.c)
     half = D // 2
     wo_rows = pl.ds(pl.multiple_of(here.y * 16, 16), 16)
@@ -563,8 +627,11 @@
     wo_place = wo.at[here.x, here.z, here.y]
     own_wo = pltpu.make_async_copy(wo_own, wo_place, near.at[1])
     own_wo.start()
-    tg[here.pos] = targets[...]
+    loads[0].wait()
+    loads[1].wait()
     local_states(keys, values, kf, state, sums)
+    for load in loads[2:]:
+        load.wait()
     await_all()
 
     def wo_peer(i):
@@ -587,59 +654,54 @@
         remote(wo_own, wo_place, zsend.at[i], zrecv.at[here.z], to).wait_send()
         return 0
 
-    lax.fori_loop(1, NZ, wo_give, 0)
+    for i in (4, 3, 5, 2, 6, 1, 7):
+        wo_give(i, 0)
     prefix = Prefix(
         here,
-        (state, sums, part, ksum, cin, kin, cout, kout, stage, kstage, state_in, sum_in),
-        (xsend, xrecv, csend, crecv, fsend, frecv),
+        (state, sums, part, ksum, below, kbelow, above, kabove, cout, kout, stage, kstage, state_in, sum_in),
+        (xsend, xrecv, usend, urecv, downsend, downrecv, fsend, frecv),
     )
+    ring = VocabRing(here, w_hbm, wv, near.at[0], rsend, rrecv, rpsend, rprecv)
+    weights = PlaneGather(here, lambda x, y, start, count: wo.at[x, pl.ds(start, count), y], WO_CUTS, psend, precv)
+    mine, theirs = attended.at[here.c], attended.at[1 - here.c]
+    rows_over = remote(mine, mine, hsend.at[0], hrecv.at[0], partner)
+
+    def give_targets(i, _):
+        slot, peer = here.plane_peer(i)
+        own = tg.at[here.pos]
+        remote(own, own, tsend.at[i], trecv.at[here.pos], peer).start()
+        return 0
+
     for copy in prefix.exchange():
         copy.start()
-    ring = VocabRing(here, w_hbm, wv, near.at[0], rsend, rrecv, rpsend, rprecv)
     ring.begin()
-
-    def give_targets(i, _):
-        slot, peer = here.plane_peer(i)
-        mine = tg.at[here.pos]
-        remote(mine, mine, tsend.at[i], trecv.at[here.pos], peer).start()
-        return 0
-
-    lax.fori_loop(1, 16, give_targets, 0)
+    inner_blocks(0, queries, kf, values, qf, probs, numer)
     for copy in prefix.exchange():
         copy.wait_recv()
-
-    @pl.when(here.y == 0)
-    def _():
-        for j in range(CHUNKS):
-            prefix.chunk(j)
-
-    inner_blocks(queries, kf, values, qf, probs, numer)
+    prefix.start()
+    inner_blocks(HALF_HEADS, queries, kf, values, qf, probs, numer)
     own_wo.wait()
     lax.fori_loop(1, NZ, wo_take, 0)
-    weights = PlaneGather(here, lambda x, y, start, count: wo.at[x, pl.ds(start * 2, count * 2), y], psend, precv)
     weights.begin_along("x")
-
-    @pl.when(here.y > 0)
-    def _():
-        for j in range(CHUNKS):
-            prefix.chunk(j)
-
+    prefix.relay()
     weights.begin_along("y")
-    weights.event(1)
+    lax.fori_loop(1, 16, give_targets, 0)
+    weights.event(1, (0,))
+    prefix.finish()
+    weights.event(1, (1,))
+    weights.event(2)
     prefix.take()
-    mine = attended.at[here.c]
     outer_blocks(0, qf, probs, numer, state_in, sum_in, mine)
-    weights.event(2)
+    ring.advance(1)
     weights.event(3)
     outer_blocks(HALF_HEADS, qf, probs, numer, state_in, sum_in, mine)
-    rows_over = remote(mine, mine, hsend.at[0], hrecv.at[0], partner)
     rows_over.start()
-    ring.advance(1)
     weights.event(4)
+    target_columns(here, tg, tcol, tsend, trecv)
     weights.event(5)
     weights.event(6)
+    ring.advance(2)
     weights.event(7)
-    theirs = attended.at[1 - here.c]
     remote(theirs, theirs, hsend.at[0], hrecv.at[0], partner).wait_recv()
     weights.event(8)
 
@@ -661,21 +723,20 @@
     projected[:, :half] = halves[0]
     projected[:, half:] = halves[1]
     normalise(projected, gain, acts.at[here.pos])
-    unit = BLOCK // 4
     gather = PlaneGather(
-        here, lambda x, y, start, count: acts.at[x * NY + y, pl.ds(start * unit, count * unit)], gsend, grecv
+        here, lambda x, y, start, count: acts.at[x * NY + y, pl.ds(start, count)], ROW_CUTS, gsend, grecv
     )
     gather.begin()
-    ring.advance(2)
     gather.event(1)
+    ring.advance(3)
     gather.event(2)
-    ring.advance(3)
     ring.advance(4)
     ring.finish_recv()
-    vocab_part(here, gather, acts, wv, tg, tcol, out_stats, in_stats, ssend, srecv, tsend, trecv)
+    vocab_part(here, gather, acts, wv, tcol, out_stats, in_stats, ssend, srecv)
     losses = losses_of(here, out_stats, in_stats, ssend, srecv)
-    loss_ref[...] = losses
-    mean_ref[...] = domain_part(here, losses, domains, dom, dsend, drecv)
+    means = domain_part(here, losses, domains, dom, dsend, drecv)
+    first = lax.broadcasted_iota(jnp.int32, (8, 128), 0) == 0
+    small[...] = jnp.where(first, losses, means)
     lax.fori_loop(1, NZ, wo_sent, 0)
     prefix.finish_send()
     weights.finish_send()
@@ -690,17 +751,20 @@
     vmem = pl.BlockSpec(memory_space=pltpu.VMEM)
     dma = pltpu.SemaphoreType.DMA
     low, wide = jnp.bfloat16, jnp.float32
-    projected, losses, means = pl.pallas_call(
+    anywhere = pl.BlockSpec(memory_space=pl.ANY)
+    projected, small = pl.pallas_call(
         whole_kernel,
         out_shape=(
             jax.ShapeDtypeStruct((BLOCK, D), low),
-            jax.ShapeDtypeStruct((1, BLOCK), wide),
-            jax.ShapeDtypeStruct((8, 128), wide),
+            jax.ShapeDtypeStruct((8, BLOCK), wide),
         ),
-        in_specs=[vmem] * 5
-        + [pl.BlockSpec(memory_space=pltpu.SMEM), pl.BlockSpec(memory_space=pl.ANY), pl.BlockSpec(memory_space=pl.ANY)],
-        out_specs=(vmem, vmem, vmem),
+        in_specs=[anywhere] * 5 + [pl.BlockSpec(memory_space=pltpu.SMEM), anywhere, anywhere],
+        out_specs=(vmem, vmem),
         scratch_shapes=[
+            pltpu.VMEM((BLOCK, D), low),
+            pltpu.VMEM((BLOCK, D), low),
+            pltpu.VMEM((BLOCK, D), low),
+            pltpu.VMEM((1, D), wide),
             pltpu.VMEM((BLOCK, D), low),
             pltpu.VMEM((BLOCK, D), low),
             pltpu.VMEM((HEADS, BLOCK, BLOCK), low),
@@ -708,6 +772,8 @@
             pltpu.VMEM((2, HALF_HEADS, HD, HD), wide),
             pltpu.VMEM((2, HALF_HEADS, 1, HD), wide),
             pltpu.VMEM((HALF_HEADS, HD, HD), wide),
+            pltpu.VMEM((HALF_HEADS, 1, HD), wide),
+            pltpu.VMEM((HALF_HEADS, HD, HD), low),
             pltpu.VMEM((HALF_HEADS, 1, HD), wide),
             pltpu.VMEM((HALF_HEADS, HD, HD), low),
             pltpu.VMEM((HALF_HEADS, 1, HD), wide),
@@ -728,9 +794,11 @@
             pltpu.VMEM((16, 8, 128), wide),
             pltpu.VMEM((16, 8, 128), wide),
             pltpu.VMEM((2, 16, 8, 128), wide),
+            dma((7,)),
             dma((2,)),
             dma((2,)),
-            dma((2,)),
+            dma((CHUNKS + 1,)),
+            dma((CHUNKS + 1,)),
             dma((CHUNKS + 1,)),
             dma((CHUNKS + 1,)),
             dma((CHUNKS + 1,)),
@@ -758,7 +826,7 @@
             collective_id=0, has_side_effects=True, vmem_limit_bytes=60 * 1024 * 1024
         ),
     )(queries[0], keys[0], values[0], norm_gain[None], targets, domains, w_out, w_vocab)
-    return (projected[None], losses, means[0, :DOMAINS])
+    return (projected[None], small[:1], small[1, :DOMAINS])
 
 
 def solution(mesh):

time: 143 us -> 133 us (0.930)
  Pallas kernels: 138 us -> 128 us
    pallas_call x1, Pallas kernels: 138 us -> 128 us  [on_device(): pl.pallas_call(whole_kernel, out_shape=(jax.ShapeDtypeStruct((BLOCK, D),...]
    unnamed x2 -> x1, local copies, waits for them, and re-layouts: 3.06 us -> 1.88 us
where the time goes in v4:
time: 133 us
  Pallas kernels  128 us (96%)
  local copies, waits for them, and re-layouts  4.25 us (3%)
    pallas_call x1, Pallas kernels, on_device(): pl.pallas_call(whole_kernel, out_shape=(jax.ShapeDtypeStruct((BLOCK, D),...  128 us

profile of v4, /device:TPU:1, one launch (start us, length us, event | category | flops | bytes accessed | tf_op | source)
XLA Modules:
  0.0 132.8 jit_solution(5691751059462340707)
XLA Ops:
  0.6 128.0 %shard_map.103 = (bf16[128,2048]{1,0:T(8,128)(2,1)}, f32[8,128]{1,0:T(8,128)}) custom-call(bf16[128,2048]{1,0:T(8,128)(2,1)} %bitcast.7, bf16[128,2048]{1,0:T(8,128)(2,1)} %bitcast.8, bf16[128,2048]{1,0:T(8,128)(2,1)} %bitcast.9, f32[1,2048]{1,0:T(1,128)} %bitcast.11, s32[1,128]{1,0:T(1,128)} %targets.1, s32[32]{0:T(128)} %domains.1, ...), custom_call_target="tpu_custom_call" | custom-call | tf_op jit(solution)/shard_map/pallas_call | solution.py:755
  128.6 1.2 slice.6
  129.8 1.2 slice_bitcast_fusion
  131.0 1.9 %copy.12 = bf16[1,128,2048]{2,1,0:T(8,128)(2,1)} copy(bf16[1,128,2048]{2,1,0:T(8,128)(2,1)} %bitcast.10) | data formatting | bytes 1048576

commit v5 on v4

--- a/solution.py
+++ b/solution.py
@@ -125,9 +125,8 @@
                 self.hop(k + 1, by, False).start()
             self.share(k, by, False).start()
 
-    def finish_recv(self):
-        self.own().wait()
-        for k in range(1, 5):
+    def finish_recv(self, *steps):
+        for k in steps:
             for by in (1, -1):
                 self.share(k, by, True).wait_recv()
 
@@ -233,17 +232,18 @@
                 self.copy(half, name, False).wait_send()
 
 
-SOURCES = (
-    ((0, 0), (-1, 0)),
-    ((1, 0), (0, -1)),
-    ((0, 1), (-1, -1)),
-    ((-1, 1), (1, -1)),
-    ((1, 1), (2, 0)),
-    ((0, 2), (2, -1)),
-    ((2, 1), (-1, 2)),
-    ((1, 2), (2, 2)),
+PIECES = (
+    ((0, 0), (0, 0), (-1, 0), (0, -1)),
+    ((1, 0), (0, 1), (0, -1), (-1, 0)),
+    ((0, 1), (1, 0), (2, 0), (0, 2)),
+    ((-1, -1), (-1, -1), (1, 1), (1, 1)),
+    ((-1, 1), (-1, 1), (1, -1), (1, -1)),
+    ((0, 2), (2, 0), (2, -1), (-1, 2)),
+    ((2, 1), (1, 2), (-1, 2), (2, -1)),
+    ((1, 2), (2, 1), (2, 2), (2, 2)),
 )
-EVENTS = ((), (3,), (4,), (), (5,), (6, 7), (), (8,))
+EVENTS = ((1,), (2,), (3,), (4,), (), (5, 6), (7,), (8,))
+NEAR = (0, -1, 1, -2, 2, -3, 3, 4)
 
 
 def pick(table, i):
@@ -253,18 +253,26 @@
     return value
 
 
-def stats_of(here, acts, wv, tcol, p1, p2):
+def stats_of(here, acts, wv, tcol, slots, before):
     rows = 2 * BLOCK
     lane = lax.broadcasted_iota(jnp.int32, (rows, 128), 1)
     whole = here.y < NY - 1
     column = jnp.minimum(here.y * TILE, SHARD - TILE)
-    wanted = jnp.concatenate([tcol[p1], tcol[p2]], axis=0) - lane.astype(jnp.float32)
+    middle = BLOCK // 2
+
+    def joined(ref):
+        return jnp.concatenate(
+            [ref[slot, (n % 2) * middle : (n % 2 + 1) * middle] for n, slot in enumerate(slots)], axis=0
+        )
+
+    wanted = joined(tcol) - lane.astype(jnp.float32)
 
     def tile(n, carry):
+        before(n)
         top, total, hit = carry
-        left = jnp.concatenate([acts[p1], acts[p2]], axis=0)
-        logits = jnp.dot(left, wv[n], preferred_element_type=jnp.float32)
-        base = ((here.x * NZ + n) * SHARD + column).astype(jnp.float32)
+        shard = lax.rem(here.z + pick(NEAR, n) + NZ, NZ)
+        logits = jnp.dot(joined(acts), wv[shard], preferred_element_type=jnp.float32)
+        base = ((here.x * NZ + shard) * SHARD + column).astype(jnp.float32)
         one, two = logits[:, :128], logits[:, 128:]
         now = jnp.maximum(top, jnp.maximum(jnp.where(whole, one, two), two))
         add = jnp.exp(one - now)
@@ -300,7 +308,22 @@
     lax.fori_loop(1, 16, take_targets, 0)
 
 
-def vocab_part(here, gather, acts, wv, tcol, out_stats, in_stats, ssend, srecv):
+def stat_copies(here, i, pair, slots, out_stats, in_stats, ssend, srecv):
+    for half in (0, 1):
+        slot = slots[2 * pair + half]
+        to = here.at(x=lax.div(slot, NY), y=lax.rem(slot, NY))
+        yield remote(
+            out_stats.at[i, pair], in_stats.at[half, here.pos], ssend.at[i, pair, half], srecv.at[half, here.pos], to
+        )
+
+
+def slots_of(here, i):
+    return [
+        here.slot(pick([four[n][0] for four in PIECES], i), pick([four[n][1] for four in PIECES], i)) for n in range(4)
+    ]
+
+
+def vocab_part(here, gather, ring, acts, wv, tcol, out_stats, in_stats, ssend, srecv):
     def batch(i, _):
         for n, events in enumerate(EVENTS):
             if events:
@@ -310,41 +333,43 @@
                     for e in events:
                         gather.event(e)
 
-        slots = []
-        for half in (0, 1):
-            dx = pick([pair[half][0] for pair in SOURCES], i)
-            dy = pick([pair[half][1] for pair in SOURCES], i)
-            slots.append(here.slot(dx, dy))
-        table = stats_of(here, acts, wv, tcol, *slots)
-        for half in (0, 1):
-            slot = slots[half]
-            out_stats[slot] = table[half * BLOCK : (half + 1) * BLOCK].T[:8]
-
-        def give(half):
-            slot = slots[half]
-            to = here.at(x=lax.div(slot, NY), y=lax.rem(slot, NY))
-            remote(out_stats.at[slot], in_stats.at[here.pos], ssend.at[slot], srecv.at[here.pos], to).start()
+        def before(n):
+            @pl.when(jnp.logical_and(i == 0, n == NZ - 1))
+            def _():
+                ring.advance(4)
+                ring.finish_recv(4)
+
+        slots = slots_of(here, i)
+        table = stats_of(here, acts, wv, tcol, slots, before)
+        for pair in (0, 1):
+            out_stats[i, pair] = table[pair * BLOCK : (pair + 1) * BLOCK].T[:8]
 
         @pl.when(i > 0)
         def _():
-            give(0)
-
-        give(1)
-        return 0
-
-    lax.fori_loop(0, len(SOURCES), batch, 0)
+            for copy in stat_copies(here, i, 0, slots, out_stats, in_stats, ssend, srecv):
+                copy.start()
+
+        for copy in stat_copies(here, i, 1, slots, out_stats, in_stats, ssend, srecv):
+            copy.start()
+        return 0
+
+    lax.fori_loop(0, len(PIECES), batch, 0)
 
 
 def losses_of(here, out_stats, in_stats, ssend, srecv):
-    in_stats[here.pos] = out_stats[here.pos]
+    for half in (0, 1):
+        in_stats[half, here.pos] = out_stats[0, 0]
 
     def take(i, _):
         slot, peer = here.plane_peer(i)
-        remote(out_stats.at[slot], in_stats.at[slot], ssend.at[slot], srecv.at[slot], peer).wait_recv()
+        for half in (0, 1):
+            place = in_stats.at[half, slot]
+            remote(place, place, ssend.at[0, 0, 0], srecv.at[half, slot], peer).wait_recv()
         return 0
 
     lax.fori_loop(1, 16, take, 0)
-    stats = [in_stats[n] for n in range(16)]
+    early = lax.broadcasted_iota(jnp.int32, (8, BLOCK), 1) < BLOCK // 2
+    stats = [jnp.where(early, in_stats[0, n], in_stats[1, n]) for n in range(16)]
     top = functools.reduce(jnp.maximum, [s[0:1] for s in stats])
     total = sum(s[1:2] * jnp.exp(s[0:1] - top) for s in stats)
     hit = sum(s[2:3] for s in stats)
@@ -383,13 +408,26 @@
 def finish_sends(here, out_stats, in_stats, ssend, srecv, tg, tsend, trecv, dom, dsend, drecv):
     def one(i, _):
         slot, peer = here.plane_peer(i)
-        remote(out_stats.at[slot], in_stats.at[slot], ssend.at[slot], srecv.at[slot], peer).wait_send()
         remote(tg.at[slot], tg.at[slot], tsend.at[i], trecv.at[slot], peer).wait_send()
         for stage in (0, 1):
             remote(dom.at[stage, slot], dom.at[stage, slot], dsend.at[stage, i], drecv.at[stage, slot], peer).wait_send()
         return 0
 
     lax.fori_loop(1, 16, one, 0)
+
+    def batch(i, _):
+        slots = slots_of(here, i)
+
+        @pl.when(i > 0)
+        def _():
+            for copy in stat_copies(here, i, 0, slots, out_stats, in_stats, ssend, srecv):
+                copy.wait_send()
+
+        for copy in stat_copies(here, i, 1, slots, out_stats, in_stats, ssend, srecv):
+            copy.wait_send()
+        return 0
+
+    lax.fori_loop(0, len(PIECES), batch, 0)
 
 
 HALF_HEADS = HEADS // 2
@@ -727,12 +765,10 @@
         here, lambda x, y, start, count: acts.at[x * NY + y, pl.ds(start, count)], ROW_CUTS, gsend, grecv
     )
     gather.begin()
-    gather.event(1)
+    ring.own().wait()
     ring.advance(3)
-    gather.event(2)
-    ring.advance(4)
-    ring.finish_recv()
-    vocab_part(here, gather, acts, wv, tcol, out_stats, in_stats, ssend, srecv)
+    ring.finish_recv(1, 2, 3)
+    vocab_part(here, gather, ring, acts, wv, tcol, out_stats, in_stats, ssend, srecv)
     losses = losses_of(here, out_stats, in_stats, ssend, srecv)
     means = domain_part(here, losses, domains, dom, dsend, drecv)
     first = lax.broadcasted_iota(jnp.int32, (8, 128), 0) == 0
@@ -745,6 +781,12 @@
     gather.finish_send()
     ring.finish_send()
     finish_sends(here, out_stats, in_stats, ssend, srecv, tg, tsend, trecv, dom, dsend, drecv)
+
+
+def outputs_kernel(projected, small, projected_out, loss_out, mean_out):
+    projected_out[...] = projected[...]
+    loss_out[...] = small[0:1]
+    mean_out[...] = small[1, :DOMAINS]
 
 
 def on_device(queries, keys, values, w_out, norm_gain, w_vocab, targets, domains):
@@ -791,8 +833,8 @@
             pltpu.VMEM((NZ, D, TILE), low),
             pltpu.VMEM((16, 1, BLOCK), jnp.int32),
             pltpu.VMEM((16, BLOCK, BLOCK), wide),
-            pltpu.VMEM((16, 8, 128), wide),
-            pltpu.VMEM((16, 8, 128), wide),
+            pltpu.VMEM((8, 2, 8, 128), wide),
+            pltpu.VMEM((2, 16, 8, 128), wide),
             pltpu.VMEM((2, 16, 8, 128), wide),
             dma((7,)),
             dma((2,)),
@@ -817,8 +859,8 @@
             dma((2, 4)),
             dma((16,)),
             dma((16,)),
-            dma((16,)),
-            dma((16,)),
+            dma((8, 2, 2)),
+            dma((2, 16)),
             dma((2, 16)),
             dma((2, 16)),
         ],
@@ -826,7 +868,17 @@
             collective_id=0, has_side_effects=True, vmem_limit_bytes=60 * 1024 * 1024
         ),
     )(queries[0], keys[0], values[0], norm_gain[None], targets, domains, w_out, w_vocab)
-    return (projected[None], small[:1], small[1, :DOMAINS])
+    projected, losses, means = pl.pallas_call(
+        outputs_kernel,
+        out_shape=(
+            jax.ShapeDtypeStruct((BLOCK, D), low),
+            jax.ShapeDtypeStruct((1, BLOCK), wide),
+            jax.ShapeDtypeStruct((DOMAINS,), wide),
+        ),
+        in_specs=[vmem, vmem],
+        out_specs=(vmem, vmem, vmem),
+    )(projected, small)
+    return (projected[None], losses, means)
 
 
 def solution(mesh):

time: 133 us -> 127 us (0.955)
  local copies, waits for them, and re-layouts: 4.25 us -> 0 us
    pallas_call x1, Pallas kernels: 128 us -> 125 us  [on_device(): pl.pallas_call(whole_kernel, out_shape=(jax.ShapeDtypeStruct((BLOCK, D),...]
    unnamed x1 -> x0, local copies, waits for them, and re-layouts: 1.88 us -> none
    pallas_call x0 -> x1, Pallas kernels: none -> 1.88 us  [on_device(): pl.pallas_call(outputs_kernel, out_shape=(jax.ShapeDtypeStruct((BLOCK, D)...]
where the time goes in v5:
time: 127 us
  Pallas kernels  127 us (100%)
    pallas_call x1, Pallas kernels, on_device(): pl.pallas_call(whole_kernel, out_shape=(jax.ShapeDtypeStruct((BLOCK, D),...  125 us

profile of v5, /device:TPU:1, one launch (start us, length us, event | category | flops | bytes accessed | tf_op | source)
XLA Modules:
  0.0 127.3 jit_solution(684546187179041469)
XLA Ops:
  0.6 124.8 %shard_map.103 = (bf16[128,2048]{1,0:T(8,128)(2,1)}, f32[8,128]{1,0:T(8,128)}) custom-call(bf16[128,2048]{1,0:T(8,128)(2,1)} %bitcast.5, bf16[128,2048]{1,0:T(8,128)(2,1)} %bitcast.6, bf16[128,2048]{1,0:T(8,128)(2,1)} %bitcast.7, f32[1,2048]{1,0:T(1,128)} %bitcast.8, s32[1,128]{1,0:T(1,128)} %targets.1, s32[32]{0:T(128)} %domains.1, ...), custom_call_target="tpu_custom_call" | custom-call | tf_op jit(solution)/shard_map/pallas_call | solution.py:797
  125.4 1.9 %shard_map.104 = (bf16[128,2048]{1,0:T(8,128)(2,1)}, f32[1,128]{1,0:T(1,128)}, f32[7]{0:T(128)}) custom-call(bf16[128,2048]{1,0:T(8,128)(2,1)} %get-tuple-element.8.projected, f32[8,128]{1,0:T(8,128)} %get-tuple-element.9.small), custom_call_target="tpu_custom_call" | custom-call | tf_op jit(solution)/shard_map/pallas_call | solution.py:871

commit v6 on v5

--- a/solution.py
+++ b/solution.py
@@ -59,6 +59,14 @@
     )
 
 
+def all_sent(ref, sem, here):
+    remote(ref, ref, sem, sem, here.at(c=1 - here.c)).wait_send()
+
+
+def all_here(ref, sem, here):
+    remote(ref, ref, sem, sem, here.at(c=1 - here.c)).wait_recv()
+
+
 def greet_all(here):
     barrier = pltpu.get_barrier_semaphore()
 
@@ -75,9 +83,9 @@
 
 
 class VocabRing:
-    def __init__(self, here, w_hbm, wv, near, send, recv, psend, precv):
+    def __init__(self, here, w_hbm, wv, near, send, recv, precv):
         self.here, self.w, self.wv, self.near = here, w_hbm, wv, near
-        self.send, self.recv, self.psend, self.precv = send, recv, psend, precv
+        self.send, self.recv, self.precv = send, recv, precv
         self.first = pl.multiple_of(here.c * (D // 2), D // 2)
         self.column = pl.multiple_of(jnp.minimum(here.y * TILE, SHARD - TILE), 128)
 
@@ -91,50 +99,40 @@
     def slot(self, off):
         return lax.rem(self.here.z + off + NZ, NZ)
 
-    def hop(self, k, by, at_receiver):
+    def hop(self, k, by):
         part = "all" if k < 4 else ("lo" if by > 0 else "hi")
-        off = -by * (k if at_receiver else k - 1)
-        dst = self.wv.at[self.slot(off), self.rows(part)]
-        src = self.w.at[self.rows(part), pl.ds(self.column, TILE)] if (k == 1 and not at_receiver) else dst
-        n = 0 if by > 0 else 1
-        return remote(src, dst, self.send.at[n, k - 1], self.recv.at[n, k - 1], self.here.step("z", by))
-
-    def share(self, k, by, at_receiver):
+        dst = self.wv.at[self.slot(-by * (k - 1)), self.rows(part)]
+        src = self.w.at[self.rows(part), pl.ds(self.column, TILE)] if k == 1 else dst
+        return remote(src, dst, self.send, self.recv.at[k - 1], self.here.step("z", by))
+
+    def share(self, k, by):
         part = "all" if k < 4 else ("lo" if by > 0 else "hi")
-        off = -by * k
-        rows = self.rows(part)
-        if at_receiver:
-            start = pl.multiple_of((1 - self.here.c) * (D // 2), D // 2)
-            rows = {"all": pl.ds(start, D // 2), "lo": pl.ds(start, D // 4), "hi": pl.ds(start + D // 4, D // 4)}[part]
-        ref = self.wv.at[self.slot(off), rows]
-        n = 0 if by > 0 else 1
-        return remote(ref, ref, self.psend.at[n, k - 1], self.precv.at[n, k - 1], self.here.at(c=1 - self.here.c))
+        ref = self.wv.at[self.slot(-by * k), self.rows(part)]
+        return remote(ref, ref, self.send, self.precv.at[k // 4], self.here.at(c=1 - self.here.c))
 
     def own(self):
         return pltpu.make_async_copy(self.w.at[:, pl.ds(self.column, TILE)], self.wv.at[self.here.z], self.near)
 
     def begin(self):
         for by in (1, -1):
-            self.hop(1, by, False).start()
+            self.hop(1, by).start()
         self.own().start()
 
     def advance(self, k):
+        all_here(self.wv.at[0] if k < 4 else self.wv.at[0, : D // 2], self.recv.at[k - 1], self.here)
         for by in (1, -1):
-            self.hop(k, by, True).wait_recv()
             if k < 4:
-                self.hop(k + 1, by, False).start()
-            self.share(k, by, False).start()
-
-    def finish_recv(self, *steps):
-        for k in steps:
-            for by in (1, -1):
-                self.share(k, by, True).wait_recv()
+                self.hop(k + 1, by).start()
+            self.share(k, by).start()
+
+    def shared(self, last):
+        if last:
+            all_here(self.wv.at[0, : D // 2], self.precv.at[1], self.here)
+        else:
+            all_here(self.wv.at[0:3], self.precv.at[0], self.here)
 
     def finish_send(self):
-        for k in range(1, 5):
-            for by in (1, -1):
-                self.hop(k, by, False).wait_send()
-                self.share(k, by, False).wait_send()
+        all_sent(self.wv.at[0:7], self.send, self.here)
 
 
 HALF = {
@@ -159,90 +157,83 @@
     "B2+l": (-2, -1, "lo", "B", 1),
     "B2-h": (2, 1, "hi", "B", -1),
 }
-ORDER = list(HALF)
+EVENT = {
+    1: (("A1+", "A1-"), ("A2+", "A2-", "B1+m", "B1-m", "B1+p", "B1-p")),
+    2: (("B1+o", "B1-o"), ("B2+o", "B2-o")),
+    3: (("A2+", "A2-"), ("B1+l", "B1-l", "B1+h", "B1-h")),
+    4: (("B1+m", "B1-m"), ("B2-m",)),
+    5: (("B1+p", "B1-p"), ("B2+p",)),
+    6: (("B2+o", "B2-o"), ()),
+    7: (("B1+l", "B1-l", "B1+h", "B1-h"), ("B2+l", "B2-h")),
+    8: (("B2+p", "B2-m"), ()),
+    9: (("B2+l", "B2-h"), ()),
+}
+EVENT_OF = {name: e for e, (names, _) in EVENT.items() for name in names}
 WO_CUTS = ((0, 1, 3), (3, 5, 8))
 ROW_CUTS = ((0, 32, 64), (64, 96, 128))
 
 
 class PlaneGather:
-    def __init__(self, here, view, cuts, send, recv):
-        self.here, self.view, self.cuts, self.send_sem, self.recv_sem = here, view, cuts, send, recv
-
-    def copy(self, half, name, at_receiver):
+    def __init__(self, here, view, cuts, amount, apart, send, recv):
+        self.here, self.view, self.cuts, self.amount, self.apart = here, view, cuts, amount, apart
+        self.send_sem, self.recv_sem = send, recv
+
+    def start(self, half, name):
         a, b, part, axis, by = HALF[name]
-        if at_receiver:
-            a, b = (a - by, b) if axis == "A" else (a, b - by)
         first, second = ("x", "y") if half == 0 else ("y", "x")
         dx, dy = (a, b) if half == 0 else (b, a)
         first_row, middle, last_row = self.cuts[half]
-        start, stop = {"all": (first_row, last_row), "lo": (first_row, middle), "hi": (middle, last_row)}[part]
+        begin, end = {"all": (first_row, last_row), "lo": (first_row, middle), "hi": (middle, last_row)}[part]
         column, row = lax.rem(self.here.x + dx + NX, NX), lax.rem(self.here.y + dy + NY, NY)
-        ref = self.view(column, row, start, stop - start)
-        n = half * len(ORDER) + ORDER.index(name)
-        return remote(
-            ref, ref, self.send_sem.at[n], self.recv_sem.at[n], self.here.step(first if axis == "A" else second, by)
-        )
+        ref = self.view(column, row, begin, end - begin)
+        to = self.here.step(first if axis == "A" else second, by)
+        remote(ref, ref, self.send_sem, self.recv_sem.at[self.index(EVENT_OF[name], half)], to).start()
+
+    def index(self, e, half):
+        return len(EVENT) if e == 1 and half == 1 and self.apart else e - 1
 
     def begin_along(self, axis):
         half = 0 if axis == "x" else 1
         for name in ("A1+", "A1-"):
-            self.copy(half, name, False).start()
+            self.start(half, name)
         for name in ("B1+o", "B1-o"):
-            self.copy(1 - half, name, False).start()
-
-    def send(self, halves, *names):
-        for name in names:
+            self.start(1 - half, name)
+
+    def begin(self):
+        self.begin_along("x")
+        self.begin_along("y")
+
+    def event(self, e, halves=(0, 1)):
+        apart = len(halves) == 1
+        all_here(self.amount(e, halves[0] if apart else None), self.recv_sem.at[self.index(e, halves[0])], self.here)
+        for name in EVENT[e][1]:
             for half in halves:
-                self.copy(half, name, False).start()
-
-    def take(self, halves, *names):
-        for name in names:
-            for half in halves:
-                self.copy(half, name, True).wait_recv()
-
-    def begin(self):
-        self.send((0, 1), "A1+", "A1-", "B1+o", "B1-o")
-
-    def event(self, e, halves=(0, 1)):
-        if e == 1:
-            self.take(halves, "A1+", "A1-")
-            self.send(halves, "A2+", "A2-", "B1+m", "B1-m", "B1+p", "B1-p")
-        elif e == 2:
-            self.take(halves, "B1+o", "B1-o")
-            self.send(halves, "B2+o", "B2-o")
-        elif e == 3:
-            self.take(halves, "A2+", "A2-")
-            self.send(halves, "B1+l", "B1-l", "B1+h", "B1-h")
-        elif e == 4:
-            self.take(halves, "B1+p", "B1-p", "B1+m", "B1-m")
-            self.send(halves, "B2+p", "B2-m")
-        elif e == 5:
-            self.take(halves, "B2+o", "B2-o")
-        elif e == 6:
-            self.take(halves, "B1+l", "B1-l", "B1+h", "B1-h")
-            self.send(halves, "B2+l", "B2-h")
-        elif e == 7:
-            self.take(halves, "B2+p", "B2-m")
-        else:
-            self.take(halves, "B2+l", "B2-h")
-
-    def finish_send(self):
-        for name in ORDER:
-            for half in (0, 1):
-                self.copy(half, name, False).wait_send()
+                self.start(half, name)
+
+
+def rows_of_event(acts, e, half):
+    blocks = {1: 2, 2: 2, 3: 1, 4: 2, 5: 2, 6: 1, 7: 2, 8: 2, 9: 1}[e]
+    return acts.at[0:blocks]
+
+
+def places_of_event(wo, e, half):
+    if half is not None:
+        return wo.at[0, 0:6, 0] if half == 0 else wo.at[0, 0:5, 0:2]
+    places = {2: 4, 3: 2, 4: 4, 5: 4, 6: 2, 7: 4, 8: 4, 9: 2}[e]
+    return wo.at[0, 0:places]
 
 
 PIECES = (
     ((0, 0), (0, 0), (-1, 0), (0, -1)),
     ((1, 0), (0, 1), (0, -1), (-1, 0)),
     ((0, 1), (1, 0), (2, 0), (0, 2)),
-    ((-1, -1), (-1, -1), (1, 1), (1, 1)),
-    ((-1, 1), (-1, 1), (1, -1), (1, -1)),
+    ((-1, -1), (-1, -1), (-1, 1), (1, -1)),
+    ((1, -1), (-1, 1), (1, 1), (1, 1)),
     ((0, 2), (2, 0), (2, -1), (-1, 2)),
     ((2, 1), (1, 2), (-1, 2), (2, -1)),
     ((1, 2), (2, 1), (2, 2), (2, 2)),
 )
-EVENTS = ((1,), (2,), (3,), (4,), (), (5, 6), (7,), (8,))
+EVENTS = ((1,), (2,), (3,), (4,), (5,), (6, 7), (8,), (9,))
 NEAR = (0, -1, 1, -2, 2, -3, 3, 4)
 
 
@@ -299,13 +290,11 @@
         tcol[slot] = wide.T
 
     def take_targets(i, _):
-        slot, peer = here.plane_peer(i)
-        remote(tg.at[slot], tg.at[slot], tsend.at[i], trecv.at[slot], peer).wait_recv()
-        columns(slot)
-        return 0
-
-    columns(here.pos)
-    lax.fori_loop(1, 16, take_targets, 0)
+        columns(i)
+        return 0
+
+    all_here(tg.at[0:15], trecv, here)
+    lax.fori_loop(0, 16, take_targets, 0)
 
 
 def stat_copies(here, i, pair, slots, out_stats, in_stats, ssend, srecv):
@@ -313,7 +302,7 @@
         slot = slots[2 * pair + half]
         to = here.at(x=lax.div(slot, NY), y=lax.rem(slot, NY))
         yield remote(
-            out_stats.at[i, pair], in_stats.at[half, here.pos], ssend.at[i, pair, half], srecv.at[half, here.pos], to
+            out_stats.at[i, pair], in_stats.at[half, here.pos], ssend, srecv, to
         )
 
 
@@ -337,7 +326,7 @@
             @pl.when(jnp.logical_and(i == 0, n == NZ - 1))
             def _():
                 ring.advance(4)
-                ring.finish_recv(4)
+                ring.shared(True)
 
         slots = slots_of(here, i)
         table = stats_of(here, acts, wv, tcol, slots, before)
@@ -360,14 +349,7 @@
     for half in (0, 1):
         in_stats[half, here.pos] = out_stats[0, 0]
 
-    def take(i, _):
-        slot, peer = here.plane_peer(i)
-        for half in (0, 1):
-            place = in_stats.at[half, slot]
-            remote(place, place, ssend.at[0, 0, 0], srecv.at[half, slot], peer).wait_recv()
-        return 0
-
-    lax.fori_loop(1, 16, take, 0)
+    all_here(in_stats.at[:, 0:15], srecv, here)
     early = lax.broadcasted_iota(jnp.int32, (8, BLOCK), 1) < BLOCK // 2
     stats = [jnp.where(early, in_stats[0, n], in_stats[1, n]) for n in range(16)]
     top = functools.reduce(jnp.maximum, [s[0:1] for s in stats])
@@ -388,16 +370,11 @@
 
         def give(i, _):
             slot, peer = peers(i)
-            remote(dom.at[stage, own], dom.at[stage, own], dsend.at[stage, i], drecv.at[stage, own], peer).start()
+            remote(dom.at[stage, own], dom.at[stage, own], dsend.at[stage], drecv.at[stage], peer).start()
             return 0
 
-        def take(i, _):
-            slot, peer = peers(i)
-            remote(dom.at[stage, slot], dom.at[stage, slot], dsend.at[stage, i], drecv.at[stage, slot], peer).wait_recv()
-            return 0
-
         lax.fori_loop(1, 16, give, 0)
-        lax.fori_loop(1, 16, take, 0)
+        all_here(dom.at[stage, 0:15], drecv.at[stage], here)
         value = sum(dom[stage, n] for n in range(16))
     counts = jnp.zeros((8, 128), jnp.float32)
     for n in range(DOCS):
@@ -405,29 +382,11 @@
     return value / jnp.maximum(counts * (NY * 2 * BLOCK), 1.0)
 
 
-def finish_sends(here, out_stats, in_stats, ssend, srecv, tg, tsend, trecv, dom, dsend, drecv):
-    def one(i, _):
-        slot, peer = here.plane_peer(i)
-        remote(tg.at[slot], tg.at[slot], tsend.at[i], trecv.at[slot], peer).wait_send()
-        for stage in (0, 1):
-            remote(dom.at[stage, slot], dom.at[stage, slot], dsend.at[stage, i], drecv.at[stage, slot], peer).wait_send()
-        return 0
-
-    lax.fori_loop(1, 16, one, 0)
-
-    def batch(i, _):
-        slots = slots_of(here, i)
-
-        @pl.when(i > 0)
-        def _():
-            for copy in stat_copies(here, i, 0, slots, out_stats, in_stats, ssend, srecv):
-                copy.wait_send()
-
-        for copy in stat_copies(here, i, 1, slots, out_stats, in_stats, ssend, srecv):
-            copy.wait_send()
-        return 0
-
-    lax.fori_loop(0, len(PIECES), batch, 0)
+def finish_sends(here, in_stats, ssend, tg, tsend, dom, dsend):
+    all_sent(in_stats.at[:, 0:15], ssend, here)
+    all_sent(tg.at[0:15], tsend, here)
+    for stage in (0, 1):
+        all_sent(dom.at[stage, 0:15], dsend.at[stage], here)
 
 
 HALF_HEADS = HEADS // 2
@@ -511,9 +470,9 @@
 
     def move(self, j, src, ksrc, dst, kdst, send, recv, to):
         heads = self.heads(j)
-        copies = [remote(src.at[heads], dst.at[heads], send.at[j], recv.at[j], to)]
+        copies = [remote(src.at[heads], dst.at[heads], send.at[0], recv.at[j], to)]
         if j == 0:
-            copies.append(remote(ksrc, kdst, send.at[CHUNKS], recv.at[CHUNKS], to))
+            copies.append(remote(ksrc, kdst, send.at[1], recv.at[CHUNKS], to))
         return copies
 
     def up(self, j):
@@ -569,10 +528,10 @@
     def give(self, j):
         heads = self.heads(j)
         there = self.state_in.at[self.here.c, heads]
-        copies = [remote(self.stage.at[heads], there, self.fsend.at[j], self.frecv.at[j], self.partner)]
+        copies = [remote(self.stage.at[heads], there, self.fsend.at[0], self.frecv.at[0], self.partner)]
         if j == 0:
             copies.append(
-                remote(self.kstage, self.sum_in.at[self.here.c], self.fsend.at[CHUNKS], self.frecv.at[CHUNKS], self.partner)
+                remote(self.kstage, self.sum_in.at[self.here.c], self.fsend.at[1], self.frecv.at[1], self.partner)
             )
         return copies
 
@@ -604,32 +563,24 @@
                 copy.start()
 
     def take(self):
-        other = 1 - self.here.c
-        for j in range(CHUNKS):
-            heads = self.heads(j)
-            remote(
-                self.stage.at[heads], self.state_in.at[other, heads], self.fsend.at[j], self.frecv.at[j], self.partner
-            ).wait_recv()
-        remote(
-            self.kstage, self.sum_in.at[other], self.fsend.at[CHUNKS], self.frecv.at[CHUNKS], self.partner
-        ).wait_recv()
+        all_here(self.stage, self.frecv.at[0], self.here)
+        all_here(self.kstage, self.frecv.at[1], self.here)
 
     def finish_send(self):
         for copy in self.exchange():
             copy.wait_send()
-        for j in range(CHUNKS):
-            for copy in self.give(j):
-                copy.wait_send()
-
-            @pl.when(self.here.y < NY - 1)
-            def _():
-                for copy in self.up(j):
-                    copy.wait_send()
-
-            @pl.when(jnp.logical_or(self.here.y == 0, self.here.y == 3))
-            def _():
-                for copy in self.down(j, False):
-                    copy.wait_send()
+        all_sent(self.stage, self.fsend.at[0], self.here)
+        all_sent(self.kstage, self.fsend.at[1], self.here)
+
+        @pl.when(self.here.y < NY - 1)
+        def _():
+            all_sent(self.cout, self.usend.at[0], self.here)
+            all_sent(self.kout, self.usend.at[1], self.here)
+
+        @pl.when(jnp.logical_or(self.here.y == 0, self.here.y == 3))
+        def _():
+            all_sent(self.above, self.dsend.at[0], self.here)
+            all_sent(self.kabove, self.dsend.at[1], self.here)
 
 
 def normalise(projected, gain, out):
@@ -648,7 +599,7 @@
     queries, keys, values, gain, qf, kf, probs, numer, state, sums, part, ksum, below, kbelow, above, kabove, cout, kout,
     stage, kstage, state_in, sum_in, attended, wo, halves, given, acts, wv, tg, tcol, out_stats, in_stats, dom,
     near, xsend, xrecv, usend, urecv, downsend, downrecv, fsend, frecv, zsend, zrecv, hsend, hrecv, psend, precv,
-    gsend, grecv, rsend, rrecv, rpsend, rprecv, tsend, trecv, ssend, srecv, dsend, drecv,
+    gsend, grecv, rsend, rrecv, rprecv, tsend, trecv, ssend, srecv, dsend, drecv,
 ):
     here = Place()
     for ref in (below, kbelow, above, kabove):
@@ -678,18 +629,7 @@
 
     def wo_give(i, _):
         z, to = wo_peer(i)
-        remote(wo_own, wo_place, zsend.at[i], zrecv.at[here.z], to).start()
-        return 0
-
-    def wo_take(i, _):
-        z, to = wo_peer(i)
-        place = wo.at[here.x, z, here.y]
-        remote(place, place, zsend.at[i], zrecv.at[z], to).wait_recv()
-        return 0
-
-    def wo_sent(i, _):
-        z, to = wo_peer(i)
-        remote(wo_own, wo_place, zsend.at[i], zrecv.at[here.z], to).wait_send()
+        remote(wo_own, wo_place, zsend, zrecv, to).start()
         return 0
 
     for i in (4, 3, 5, 2, 6, 1, 7):
@@ -699,15 +639,18 @@
         (state, sums, part, ksum, below, kbelow, above, kabove, cout, kout, stage, kstage, state_in, sum_in),
         (xsend, xrecv, usend, urecv, downsend, downrecv, fsend, frecv),
     )
-    ring = VocabRing(here, w_hbm, wv, near.at[0], rsend, rrecv, rpsend, rprecv)
-    weights = PlaneGather(here, lambda x, y, start, count: wo.at[x, pl.ds(start, count), y], WO_CUTS, psend, precv)
+    ring = VocabRing(here, w_hbm, wv, near.at[0], rsend, rrecv, rprecv)
+    weights = PlaneGather(
+        here, lambda x, y, start, count: wo.at[x, pl.ds(start, count), y],
+        WO_CUTS, functools.partial(places_of_event, wo), True, psend, precv,
+    )
     mine, theirs = attended.at[here.c], attended.at[1 - here.c]
     rows_over = remote(mine, mine, hsend.at[0], hrecv.at[0], partner)
 
     def give_targets(i, _):
         slot, peer = here.plane_peer(i)
         own = tg.at[here.pos]
-        remote(own, own, tsend.at[i], trecv.at[here.pos], peer).start()
+        remote(own, own, tsend, trecv, peer).start()
         return 0
 
     for copy in prefix.exchange():
@@ -719,7 +662,7 @@
     prefix.start()
     inner_blocks(HALF_HEADS, queries, kf, values, qf, probs, numer)
     own_wo.wait()
-    lax.fori_loop(1, NZ, wo_take, 0)
+    all_here(wo.at[0, 0:7, 0], zrecv, here)
     weights.begin_along("x")
     prefix.relay()
     weights.begin_along("y")
@@ -738,10 +681,11 @@
     target_columns(here, tg, tcol, tsend, trecv)
     weights.event(5)
     weights.event(6)
+    weights.event(7)
     ring.advance(2)
-    weights.event(7)
+    weights.event(8)
     remote(theirs, theirs, hsend.at[0], hrecv.at[0], partner).wait_recv()
-    weights.event(8)
+    weights.event(9)
 
     def project(n, _):
         cols = pl.ds(pl.multiple_of(n * TILE, TILE), TILE)
@@ -762,25 +706,26 @@
     projected[:, half:] = halves[1]
     normalise(projected, gain, acts.at[here.pos])
     gather = PlaneGather(
-        here, lambda x, y, start, count: acts.at[x * NY + y, pl.ds(start, count)], ROW_CUTS, gsend, grecv
+        here, lambda x, y, start, count: acts.at[x * NY + y, pl.ds(start, count)],
+        ROW_CUTS, functools.partial(rows_of_event, acts), False, gsend, grecv,
     )
     gather.begin()
     ring.own().wait()
     ring.advance(3)
-    ring.finish_recv(1, 2, 3)
+    ring.shared(False)
     vocab_part(here, gather, ring, acts, wv, tcol, out_stats, in_stats, ssend, srecv)
     losses = losses_of(here, out_stats, in_stats, ssend, srecv)
     means = domain_part(here, losses, domains, dom, dsend, drecv)
     first = lax.broadcasted_iota(jnp.int32, (8, 128), 0) == 0
     small[...] = jnp.where(first, losses, means)
-    lax.fori_loop(1, NZ, wo_sent, 0)
+    all_sent(wo.at[0, 0:7, 0], zsend, here)
     prefix.finish_send()
-    weights.finish_send()
+    all_sent(acts.at[0:15, 0:64], psend, here)
     rows_over.wait_send()
     back.wait_send()
-    gather.finish_send()
+    all_sent(acts.at[0:15], gsend, here)
     ring.finish_send()
-    finish_sends(here, out_stats, in_stats, ssend, srecv, tg, tsend, trecv, dom, dsend, drecv)
+    finish_sends(here, in_stats, ssend, tg, tsend, dom, dsend)
 
 
 def outputs_kernel(projected, small, projected_out, loss_out, mean_out):
@@ -839,30 +784,29 @@
             dma((7,)),
             dma((2,)),
             dma((2,)),
+            dma((2,)),
             dma((CHUNKS + 1,)),
+            dma((2,)),
             dma((CHUNKS + 1,)),
-            dma((CHUNKS + 1,)),
-            dma((CHUNKS + 1,)),
-            dma((CHUNKS + 1,)),
-            dma((CHUNKS + 1,)),
-            dma((NZ,)),
-            dma((NZ,)),
-            dma((2,)),
-            dma((2,)),
-            dma((40,)),
-            dma((40,)),
-            dma((40,)),
-            dma((40,)),
-            dma((2, 4)),
-            dma((2, 4)),
-            dma((2, 4)),
-            dma((2, 4)),
-            dma((16,)),
-            dma((16,)),
-            dma((8, 2, 2)),
-            dma((2, 16)),
-            dma((2, 16)),
-            dma((2, 16)),
+            dma((2,)),
+            dma((2,)),
+            dma(()),
+            dma(()),
+            dma((2,)),
+            dma((2,)),
+            dma(()),
+            dma((len(EVENT) + 1,)),
+            dma(()),
+            dma((len(EVENT),)),
+            dma(()),
+            dma((4,)),
+            dma((2,)),
+            dma(()),
+            dma(()),
+            dma(()),
+            dma(()),
+            dma((2,)),
+            dma((2,)),
         ],
         compiler_params=pltpu.CompilerParams(
             collective_id=0, has_side_effects=True, vmem_limit_bytes=60 * 1024 * 1024

time: 127 us -> 124 us (0.976)
  Pallas kernels: 127 us -> 123 us
    pallas_call x1, Pallas kernels: 125 us -> 121 us  [on_device(): pl.pallas_call(whole_kernel, out_shape=(jax.ShapeDtypeStruct((BLOCK, D),...]
where the time goes in v6:
time: 124 us
  Pallas kernels  123 us (99%)
    pallas_call x1, Pallas kernels, on_device(): pl.pallas_call(whole_kernel, out_shape=(jax.ShapeDtypeStruct((BLOCK, D),...  121 us

profile of v6, /device:TPU:1, one launch (start us, length us, event | category | flops | bytes accessed | tf_op | source)
XLA Modules:
  0.0 123.9 jit_solution(11454442392028491519)
XLA Ops:
  0.6 121.4 %shard_map.103 = (bf16[128,2048]{1,0:T(8,128)(2,1)}, f32[8,128]{1,0:T(8,128)}) custom-call(bf16[128,2048]{1,0:T(8,128)(2,1)} %bitcast.5, bf16[128,2048]{1,0:T(8,128)(2,1)} %bitcast.6, bf16[128,2048]{1,0:T(8,128)(2,1)} %bitcast.7, f32[1,2048]{1,0:T(1,128)} %bitcast.8, s32[1,128]{1,0:T(1,128)} %targets.1, s32[32]{0:T(128)} %domains.1, ...), custom_call_target="tpu_custom_call" | custom-call | tf_op jit(solution)/shard_map/pallas_call | solution.py:742
  122.0 1.9 %shard_map.104 = (bf16[128,2048]{1,0:T(8,128)(2,1)}, f32[1,128]{1,0:T(1,128)}, f32[7]{0:T(128)}) custom-call(bf16[128,2048]{1,0:T(8,128)(2,1)} %get-tuple-element.8.projected, f32[8,128]{1,0:T(8,128)} %get-tuple-element.9.small), custom_call_target="tpu_custom_call" | custom-call | tf_op jit(solution)/shard_map/pallas_call | solution.py:815

commit v7 on v6

--- a/solution.py
+++ b/solution.py
@@ -169,7 +169,7 @@
     9: (("B2+l", "B2-h"), ()),
 }
 EVENT_OF = {name: e for e, (names, _) in EVENT.items() for name in names}
-WO_CUTS = ((0, 1, 3), (3, 5, 8))
+WO_CUTS = ((5, 6, 8), (0, 2, 5))
 ROW_CUTS = ((0, 32, 64), (64, 96, 128))
 
 
@@ -233,7 +233,7 @@
     ((2, 1), (1, 2), (-1, 2), (2, -1)),
     ((1, 2), (2, 1), (2, 2), (2, 2)),
 )
-EVENTS = ((1,), (2,), (3,), (4,), (5,), (6, 7), (8,), (9,))
+EVENTS = ((1, 2), (3,), (), (4,), (5,), (6, 7), (8,), (9,))
 NEAR = (0, -1, 1, -2, 2, -3, 3, 4)
 
 
@@ -244,7 +244,7 @@
     return value
 
 
-def stats_of(here, acts, wv, tcol, slots, before):
+def stats_of(here, acts, wv, tcol, slots):
     rows = 2 * BLOCK
     lane = lax.broadcasted_iota(jnp.int32, (rows, 128), 1)
     whole = here.y < NY - 1
@@ -259,9 +259,8 @@
     wanted = joined(tcol) - lane.astype(jnp.float32)
 
     def tile(n, carry):
-        before(n)
         top, total, hit = carry
-        shard = lax.rem(here.z + pick(NEAR, n) + NZ, NZ)
+        shard = lax.rem(here.z + NEAR[n] + NZ, NZ)
         logits = jnp.dot(joined(acts), wv[shard], preferred_element_type=jnp.float32)
         base = ((here.x * NZ + shard) * SHARD + column).astype(jnp.float32)
         one, two = logits[:, :128], logits[:, 128:]
@@ -272,12 +271,14 @@
         hit = hit + jnp.where(wanted == base + 128.0, two, 0.0)
         return now, total, hit
 
-    start = (
+    carry = (
         jnp.full((rows, 128), -jnp.inf, jnp.float32),
         jnp.zeros((rows, 128), jnp.float32),
         jnp.zeros((rows, 128), jnp.float32),
     )
-    top, total, hit = lax.fori_loop(0, NZ, tile, start)
+    for n in range(NZ):
+        carry = tile(n, carry)
+    top, total, hit = carry
     peak = jnp.max(top, axis=1, keepdims=True)
     total = jnp.sum(total * jnp.exp(top - peak), axis=1, keepdims=True)
     hit = jnp.sum(hit, axis=1, keepdims=True)
@@ -321,15 +322,12 @@
                 def _():
                     for e in events:
                         gather.event(e)
-
-        def before(n):
-            @pl.when(jnp.logical_and(i == 0, n == NZ - 1))
-            def _():
-                ring.advance(4)
-                ring.shared(True)
+                    if n == 0:
+                        ring.advance(4)
+                        ring.shared(True)
 
         slots = slots_of(here, i)
-        table = stats_of(here, acts, wv, tcol, slots, before)
+        table = stats_of(here, acts, wv, tcol, slots)
         for pair in (0, 1):
             out_stats[i, pair] = table[pair * BLOCK : (pair + 1) * BLOCK].T[:8]
 
@@ -401,6 +399,15 @@
 
 def head_slice(h):
     return pl.ds(pl.multiple_of(h * HD, HD), HD)
+
+
+def by_four(one, count):
+    def turn(t, _):
+        for n in range(4):
+            one(t * 4 + n, 0)
+        return 0
+
+    lax.fori_loop(0, count // 4, turn, 0)
 
 
 def local_states(keys, values, kf, state, sums):
@@ -415,7 +422,7 @@
         sums[group, n] = jnp.sum(feat.astype(jnp.float32), axis=0, keepdims=True)
         return 0
 
-    lax.fori_loop(0, HEADS, one, 0)
+    by_four(one, HEADS)
 
 
 def inner_blocks(first, queries, kf, values, qf, probs, numer):
@@ -433,7 +440,7 @@
         numer[:, cols] = jnp.dot(prob, values[:, cols], preferred_element_type=jnp.float32)
         return 0
 
-    lax.fori_loop(0, HALF_HEADS, one, 0)
+    by_four(one, HALF_HEADS)
 
 
 def outer_blocks(first, qf, probs, numer, state_in, sum_in, out):
@@ -447,7 +454,7 @@
         out[:, cols] = (top / jnp.sum(below, axis=1, keepdims=True)).astype(jnp.bfloat16)
         return 0
 
-    lax.fori_loop(0, HALF_HEADS, one, 0)
+    by_four(one, HALF_HEADS)
 
 
 class Prefix:
@@ -613,33 +620,26 @@
     half = D // 2
     wo_rows = pl.ds(pl.multiple_of(here.y * 16, 16), 16)
     wo_own = wo_hbm.at[wo_rows, pl.ds(pl.multiple_of(here.c * half, half), half)]
-    wo_place = wo.at[here.x, here.z, here.y]
+    wo_place = wo.at[here.x, 0, here.y]
     own_wo = pltpu.make_async_copy(wo_own, wo_place, near.at[1])
     own_wo.start()
+
+    ring = VocabRing(here, w_hbm, wv, near.at[0], rsend, rrecv, rprecv)
     loads[0].wait()
     loads[1].wait()
     local_states(keys, values, kf, state, sums)
     for load in loads[2:]:
         load.wait()
     await_all()
-
-    def wo_peer(i):
-        z = lax.rem(here.z + i, NZ)
-        return z, here.at(z=z)
-
-    def wo_give(i, _):
-        z, to = wo_peer(i)
-        remote(wo_own, wo_place, zsend, zrecv, to).start()
-        return 0
-
-    for i in (4, 3, 5, 2, 6, 1, 7):
-        wo_give(i, 0)
+    for i in (2, 6, 1, 7, 4, 3, 5):
+        place = NEAR.index(-i if i < 4 else NZ - i)
+        to = here.at(z=lax.rem(here.z + i, NZ))
+        remote(wo_own, wo.at[here.x, place, here.y], zsend, zrecv.at[0 if place < 5 else 1], to).start()
     prefix = Prefix(
         here,
         (state, sums, part, ksum, below, kbelow, above, kabove, cout, kout, stage, kstage, state_in, sum_in),
         (xsend, xrecv, usend, urecv, downsend, downrecv, fsend, frecv),
     )
-    ring = VocabRing(here, w_hbm, wv, near.at[0], rsend, rrecv, rprecv)
     weights = PlaneGather(
         here, lambda x, y, start, count: wo.at[x, pl.ds(start, count), y],
         WO_CUTS, functools.partial(places_of_event, wo), True, psend, precv,
@@ -655,21 +655,44 @@
 
     for copy in prefix.exchange():
         copy.start()
-    ring.begin()
     inner_blocks(0, queries, kf, values, qf, probs, numer)
     for copy in prefix.exchange():
         copy.wait_recv()
     prefix.start()
     inner_blocks(HALF_HEADS, queries, kf, values, qf, probs, numer)
     own_wo.wait()
-    all_here(wo.at[0, 0:7, 0], zrecv, here)
-    weights.begin_along("x")
+    all_here(wo.at[0, 0:4, 0], zrecv.at[0], here)
+    weights.start(1, "B1+o")
+    weights.start(1, "B1-o")
+
+    @pl.when(here.y != 2)
+    def _():
+        weights.start(1, "A1+")
+
+    @pl.when(here.y != 3)
+    def _():
+        weights.start(1, "A1-")
+
     prefix.relay()
-    weights.begin_along("y")
+
+    @pl.when(here.y == 2)
+    def _():
+        weights.start(1, "A1+")
+
+    @pl.when(here.y == 3)
+    def _():
+        weights.start(1, "A1-")
+
+    ring.begin()
+    all_here(wo.at[0, 0:3, 0], zrecv.at[1], here)
+    weights.start(0, "A1+")
+    weights.start(0, "A1-")
+    weights.start(0, "B1+o")
+    weights.start(0, "B1-o")
     lax.fori_loop(1, 16, give_targets, 0)
+    weights.event(1, (1,))
     weights.event(1, (0,))
     prefix.finish()
-    weights.event(1, (1,))
     weights.event(2)
     prefix.take()
     outer_blocks(0, qf, probs, numer, state_in, sum_in, mine)
@@ -687,21 +710,23 @@
     remote(theirs, theirs, hsend.at[0], hrecv.at[0], partner).wait_recv()
     weights.event(9)
 
+    order = [pick((0, 2, 4, 6, 7, 5, 3, 1), lax.rem(n - here.z + NZ, NZ)) for n in range(NZ)]
+
     def project(n, _):
         cols = pl.ds(pl.multiple_of(n * TILE, TILE), TILE)
         rows = jnp.concatenate([attended[0], attended[1]], axis=0)
-        w = wo[:, :, :, :, cols].reshape(D, TILE)
+        w = jnp.concatenate(
+            [wo[x, place, :, :, cols].reshape(NY * 16, TILE) for x in range(NX) for place in order], axis=0
+        )
         both = jnp.dot(rows, w, preferred_element_type=jnp.float32).astype(jnp.bfloat16)
         low = here.c == 0
         halves[here.c, :, cols] = jnp.where(low, both[:BLOCK], both[BLOCK:])
         given[:, cols] = jnp.where(low, both[BLOCK:], both[:BLOCK])
+        remote(given.at[:, cols], halves.at[here.c, :, cols], hsend.at[1], hrecv.at[1], partner).start()
         return 0
 
     lax.fori_loop(0, half // TILE, project, 0)
-    back = remote(given, halves.at[here.c], hsend.at[1], hrecv.at[1], partner)
-    back.start()
-    other = halves.at[1 - here.c]
-    remote(given, other, hsend.at[1], hrecv.at[1], partner).wait_recv()
+    all_here(given, hrecv.at[1], here)
     projected[:, :half] = halves[0]
     projected[:, half:] = halves[1]
     normalise(projected, gain, acts.at[here.pos])
@@ -722,7 +747,7 @@
     prefix.finish_send()
     all_sent(acts.at[0:15, 0:64], psend, here)
     rows_over.wait_send()
-    back.wait_send()
+    all_sent(given, hsend.at[1], here)
     all_sent(acts.at[0:15], gsend, here)
     ring.finish_send()
     finish_sends(here, in_stats, ssend, tg, tsend, dom, dsend)
@@ -791,7 +816,7 @@
             dma((2,)),
             dma((2,)),
             dma(()),
-            dma(()),
+            dma((2,)),
             dma((2,)),
             dma((2,)),
             dma(()),

time: 124 us -> 120 us (0.968)
  Pallas kernels: 123 us -> 119 us
    pallas_call x1, Pallas kernels: 121 us -> 118 us  [on_device(): pl.pallas_call(whole_kernel, out_shape=(jax.ShapeDtypeStruct((BLOCK, D),...]
where the time goes in v7:
time: 120 us
  Pallas kernels  119 us (99%)
    pallas_call x1, Pallas kernels, on_device(): pl.pallas_call(whole_kernel, out_shape=(jax.ShapeDtypeStruct((BLOCK, D),...  118 us

profile of v7, /device:TPU:1, one launch (start us, length us, event | category | flops | bytes accessed | tf_op | source)
XLA Modules:
  0.0 120.1 jit_solution(6883328018662755392)
XLA Ops:
  0.6 117.6 %shard_map.103 = (bf16[128,2048]{1,0:T(8,128)(2,1)}, f32[8,128]{1,0:T(8,128)}) custom-call(bf16[128,2048]{1,0:T(8,128)(2,1)} %bitcast.5, bf16[128,2048]{1,0:T(8,128)(2,1)} %bitcast.6, bf16[128,2048]{1,0:T(8,128)(2,1)} %bitcast.7, f32[1,2048]{1,0:T(1,128)} %bitcast.8, s32[1,128]{1,0:T(1,128)} %targets.1, s32[32]{0:T(128)} %domains.1, ...), custom_call_target="tpu_custom_call" | custom-call | tf_op jit(solution)/shard_map/pallas_call | solution.py:767
  118.3 1.9 %shard_map.104 = (bf16[128,2048]{1,0:T(8,128)(2,1)}, f32[1,128]{1,0:T(1,128)}, f32[7]{0:T(128)}) custom-call(bf16[128,2048]{1,0:T(8,128)(2,1)} %get-tuple-element.8.projected, f32[8,128]{1,0:T(8,128)} %get-tuple-element.9.small), custom_call_target="tpu_custom_call" | custom-call | tf_op jit(solution)/shard_map/pallas_call | solution.py:840

commit v8 on v7

--- a/solution.py
+++ b/solution.py
@@ -233,7 +233,7 @@
     ((2, 1), (1, 2), (-1, 2), (2, -1)),
     ((1, 2), (2, 1), (2, 2), (2, 2)),
 )
-EVENTS = ((1, 2), (3,), (), (4,), (5,), (6, 7), (8,), (9,))
+EVENTS = ((1, 2, 3), (), (4,), (5,), (), (6, 7), (8,), (9,))
 NEAR = (0, -1, 1, -2, 2, -3, 3, 4)
 
 
@@ -322,7 +322,10 @@
                 def _():
                     for e in events:
                         gather.event(e)
+                        if e == 1:
+                            ring.advance(3)
                     if n == 0:
+                        ring.shared(False)
                         ring.advance(4)
                         ring.shared(True)
 
@@ -631,10 +634,13 @@
     for load in loads[2:]:
         load.wait()
     await_all()
-    for i in (2, 6, 1, 7, 4, 3, 5):
-        place = NEAR.index(-i if i < 4 else NZ - i)
-        to = here.at(z=lax.rem(here.z + i, NZ))
-        remote(wo_own, wo.at[here.x, place, here.y], zsend, zrecv.at[0 if place < 5 else 1], to).start()
+    def wo_give(*steps):
+        for i in steps:
+            place = NEAR.index(-i if i < 4 else NZ - i)
+            to = here.at(z=lax.rem(here.z + i, NZ))
+            remote(wo_own, wo.at[here.x, place, here.y], zsend, zrecv.at[0 if place < 5 else 1], to).start()
+
+    wo_give(2, 6, 1, 7)
     prefix = Prefix(
         here,
         (state, sums, part, ksum, below, kbelow, above, kabove, cout, kout, stage, kstage, state_in, sum_in),
@@ -659,31 +665,16 @@
     for copy in prefix.exchange():
         copy.wait_recv()
     prefix.start()
+    wo_give(4, 3, 5)
+    ring.begin()
     inner_blocks(HALF_HEADS, queries, kf, values, qf, probs, numer)
     own_wo.wait()
     all_here(wo.at[0, 0:4, 0], zrecv.at[0], here)
     weights.start(1, "B1+o")
     weights.start(1, "B1-o")
-
-    @pl.when(here.y != 2)
-    def _():
-        weights.start(1, "A1+")
-
-    @pl.when(here.y != 3)
-    def _():
-        weights.start(1, "A1-")
-
+    weights.start(1, "A1+")
+    weights.start(1, "A1-")
     prefix.relay()
-
-    @pl.when(here.y == 2)
-    def _():
-        weights.start(1, "A1+")
-
-    @pl.when(here.y == 3)
-    def _():
-        weights.start(1, "A1-")
-
-    ring.begin()
     all_here(wo.at[0, 0:3, 0], zrecv.at[1], here)
     weights.start(0, "A1+")
     weights.start(0, "A1-")
@@ -692,12 +683,12 @@
     lax.fori_loop(1, 16, give_targets, 0)
     weights.event(1, (1,))
     weights.event(1, (0,))
+    weights.event(2)
+    ring.advance(1)
+    weights.event(3)
     prefix.finish()
-    weights.event(2)
     prefix.take()
     outer_blocks(0, qf, probs, numer, state_in, sum_in, mine)
-    ring.advance(1)
-    weights.event(3)
     outer_blocks(HALF_HEADS, qf, probs, numer, state_in, sum_in, mine)
     rows_over.start()
     weights.event(4)
@@ -705,7 +696,6 @@
     weights.event(5)
     weights.event(6)
     weights.event(7)
-    ring.advance(2)
     weights.event(8)
     remote(theirs, theirs, hsend.at[0], hrecv.at[0], partner).wait_recv()
     weights.event(9)
@@ -736,8 +726,7 @@
     )
     gather.begin()
     ring.own().wait()
-    ring.advance(3)
-    ring.shared(False)
+    ring.advance(2)
     vocab_part(here, gather, ring, acts, wv, tcol, out_stats, in_stats, ssend, srecv)
     losses = losses_of(here, out_stats, in_stats, ssend, srecv)
     means = domain_part(here, losses, domains, dom, dsend, drecv)

time: 120 us -> 119 us (level)
    pallas_call x1, Pallas kernels: 118 us -> 116 us  [on_device(): pl.pallas_call(whole_kernel, out_shape=(jax.ShapeDtypeStruct((BLOCK, D),...]
where the time goes in v8:
time: 119 us
  Pallas kernels  118 us (99%)
    pallas_call x1, Pallas kernels, on_device(): pl.pallas_call(whole_kernel, out_shape=(jax.ShapeDtypeStruct((BLOCK, D),...  116 us

profile of v8, /device:TPU:1, one launch (start us, length us, event | category | flops | bytes accessed | tf_op | source)
XLA Modules:
  0.0 118.8 jit_solution(4816723021158199140)
XLA Ops:
  0.6 116.3 %shard_map.103 = (bf16[128,2048]{1,0:T(8,128)(2,1)}, f32[8,128]{1,0:T(8,128)}) custom-call(bf16[128,2048]{1,0:T(8,128)(2,1)} %bitcast.5, bf16[128,2048]{1,0:T(8,128)(2,1)} %bitcast.6, bf16[128,2048]{1,0:T(8,128)(2,1)} %bitcast.7, f32[1,2048]{1,0:T(1,128)} %bitcast.8, s32[1,128]{1,0:T(1,128)} %targets.1, s32[32]{0:T(128)} %domains.1, ...), custom_call_target="tpu_custom_call" | custom-call | tf_op jit(solution)/shard_map/pallas_call | solution.py:756
  116.9 1.9 %shard_map.104 = (bf16[128,2048]{1,0:T(8,128)(2,1)}, f32[1,128]{1,0:T(1,128)}, f32[7]{0:T(128)}) custom-call(bf16[128,2048]{1,0:T(8,128)(2,1)} %get-tuple-element.8.projected, f32[8,128]{1,0:T(8,128)} %get-tuple-element.9.small), custom_call_target="tpu_custom_call" | custom-call | tf_op jit(solution)/shard_map/pallas_call | solution.py:829

commit v9 on v8

--- a/solution.py
+++ b/solution.py
@@ -19,6 +19,18 @@
 MESH = pl.DeviceIdType.MESH
 
 
+def around(count):
+    return [(n + count // 2 - 1) % count - (count // 2 - 1) for n in range(count)]
+
+
+PLANE = sorted(
+    ((dx, dy) for dx in around(NX) for dy in around(NY) if (dx, dy) != (0, 0)), key=lambda at: -abs(at[0]) - abs(at[1])
+)
+COLUMN = sorted(
+    ((dz, dc) for dz in around(NZ) for dc in (0, 1) if (dz, dc) != (0, 0)), key=lambda at: -2 * abs(at[0]) - at[1]
+)
+
+
 class Place:
     def __init__(self):
         seq, doc = lax.axis_index("seq"), lax.axis_index("doc")
@@ -47,10 +59,11 @@
         other = lax.rem(self.pos + i, NX * NY)
         return other, self.at(x=lax.div(other, NY), y=lax.rem(other, NY))
 
-    def column_peer(self, i):
-        mine = self.z * 2 + self.c
-        other = lax.rem(mine + i, NZ * 2)
-        return other, self.at(z=lax.div(other, 2), c=lax.rem(other, 2))
+    def plane_at(self, dx, dy):
+        return self.at(x=lax.rem(self.x + dx + NX, NX), y=lax.rem(self.y + dy + NY, NY))
+
+    def column_at(self, dz, dc):
+        return self.at(z=lax.rem(self.z + dz + NZ, NZ), c=lax.rem(self.c + dc, 2))
 
 
 def remote(src, dst, send, recv, to):
@@ -70,12 +83,9 @@
 def greet_all(here):
     barrier = pltpu.get_barrier_semaphore()
 
-    def greet(i, _):
-        pl.semaphore_signal(barrier, 1, device_id=here.plane_peer(i)[1], device_id_type=MESH)
-        pl.semaphore_signal(barrier, 1, device_id=here.column_peer(i)[1], device_id_type=MESH)
-        return 0
-
-    lax.fori_loop(1, 16, greet, 0)
+    for near, far in zip(PLANE, COLUMN):
+        pl.semaphore_signal(barrier, 1, device_id=here.column_at(*far), device_id_type=MESH)
+        pl.semaphore_signal(barrier, 1, device_id=here.plane_at(*near), device_id_type=MESH)
 
 
 def await_all():
@@ -365,16 +375,11 @@
     value = jnp.broadcast_to(jnp.sum(losses, axis=1, keepdims=True), (8, 128))
     value = jnp.where(lane == mine, value, 0.0)
     for stage in (0, 1):
-        peers = here.plane_peer if stage == 0 else here.column_peer
+        peers = [here.plane_at(*at) for at in PLANE] if stage == 0 else [here.column_at(*at) for at in COLUMN]
         own = here.pos if stage == 0 else here.z * 2 + here.c
         dom[stage, own] = value
-
-        def give(i, _):
-            slot, peer = peers(i)
+        for peer in peers:
             remote(dom.at[stage, own], dom.at[stage, own], dsend.at[stage], drecv.at[stage], peer).start()
-            return 0
-
-        lax.fori_loop(1, 16, give, 0)
         all_here(dom.at[stage, 0:15], drecv.at[stage], here)
         value = sum(dom[stage, n] for n in range(16))
     counts = jnp.zeros((8, 128), jnp.float32)
@@ -605,8 +610,8 @@
 
 
 def whole_kernel(
-    q_hbm, k_hbm, v_hbm, gain_hbm, targets, domains, wo_hbm, w_hbm, projected, small,
-    queries, keys, values, gain, qf, kf, probs, numer, state, sums, part, ksum, below, kbelow, above, kabove, cout, kout,
+    q_hbm, k_hbm, v_hbm, gain_hbm, targets, domains_hbm, wo_hbm, w_hbm, projected, small,
+    queries, keys, values, gain, domains, qf, kf, probs, numer, state, sums, part, ksum, below, kbelow, above, kabove, cout, kout,
     stage, kstage, state_in, sum_in, attended, wo, halves, given, acts, wv, tg, tcol, out_stats, in_stats, dom,
     near, xsend, xrecv, usend, urecv, downsend, downrecv, fsend, frecv, zsend, zrecv, hsend, hrecv, psend, precv,
     gsend, grecv, rsend, rrecv, rprecv, tsend, trecv, ssend, srecv, dsend, drecv,
@@ -614,11 +619,14 @@
     here = Place()
     for ref in (below, kbelow, above, kabove):
         ref[...] = jnp.zeros_like(ref)
-    greet_all(here)
-    moves = ((k_hbm, keys), (v_hbm, values), (q_hbm, queries), (gain_hbm, gain), (targets, tg.at[here.pos]))
+    moves = (
+        (k_hbm, keys), (v_hbm, values), (q_hbm, queries), (gain_hbm, gain), (targets, tg.at[here.pos]),
+        (domains_hbm, domains),
+    )
     loads = [pltpu.make_async_copy(src, dst, near.at[2 + n]) for n, (src, dst) in enumerate(moves)]
     for load in loads:
         load.start()
+    greet_all(here)
     partner = here.at(c=1 - here.c)
     half = D // 2
     wo_rows = pl.ds(pl.multiple_of(here.y * 16, 16), 16)
@@ -716,6 +724,7 @@
         return 0
 
     lax.fori_loop(0, half // TILE, project, 0)
+    ring.advance(2)
     all_here(given, hrecv.at[1], here)
     projected[:, :half] = halves[0]
     projected[:, half:] = halves[1]
@@ -726,7 +735,6 @@
     )
     gather.begin()
     ring.own().wait()
-    ring.advance(2)
     vocab_part(here, gather, ring, acts, wv, tcol, out_stats, in_stats, ssend, srecv)
     losses = losses_of(here, out_stats, in_stats, ssend, srecv)
     means = domain_part(here, losses, domains, dom, dsend, drecv)
@@ -759,13 +767,14 @@
             jax.ShapeDtypeStruct((BLOCK, D), low),
             jax.ShapeDtypeStruct((8, BLOCK), wide),
         ),
-        in_specs=[anywhere] * 5 + [pl.BlockSpec(memory_space=pltpu.SMEM), anywhere, anywhere],
+        in_specs=[anywhere] * 8,
         out_specs=(vmem, vmem),
         scratch_shapes=[
             pltpu.VMEM((BLOCK, D), low),
             pltpu.VMEM((BLOCK, D), low),
             pltpu.VMEM((BLOCK, D), low),
             pltpu.VMEM((1, D), wide),
+            pltpu.SMEM((DOCS,), jnp.int32),
             pltpu.VMEM((BLOCK, D), low),
             pltpu.VMEM((BLOCK, D), low),
             pltpu.VMEM((HEADS, BLOCK, BLOCK), low),
@@ -795,7 +804,7 @@
             pltpu.VMEM((8, 2, 8, 128), wide),
             pltpu.VMEM((2, 16, 8, 128), wide),
             pltpu.VMEM((2, 16, 8, 128), wide),
-            dma((7,)),
+            dma((8,)),
             dma((2,)),
             dma((2,)),
             dma((2,)),

time: 119 us -> 117 us (0.983)
    pallas_call x1, Pallas kernels: 116 us -> 115 us  [on_device(): pl.pallas_call(whole_kernel, out_shape=(jax.ShapeDtypeStruct((BLOCK, D),...]
where the time goes in v9:
time: 117 us
  Pallas kernels  117 us (100%)
    pallas_call x1, Pallas kernels, on_device(): pl.pallas_call(whole_kernel, out_shape=(jax.ShapeDtypeStruct((BLOCK, D),...  115 us

profile of v9, /device:TPU:1, one launch (start us, length us, event | category | flops | bytes accessed | tf_op | source)
XLA Modules:
  0.0 117.2 jit_solution(11508130491079159080)
XLA Ops:
  0.6 114.7 %shard_map.103 = (bf16[128,2048]{1,0:T(8,128)(2,1)}, f32[8,128]{1,0:T(8,128)}) custom-call(bf16[128,2048]{1,0:T(8,128)(2,1)} %bitcast.5, bf16[128,2048]{1,0:T(8,128)(2,1)} %bitcast.6, bf16[128,2048]{1,0:T(8,128)(2,1)} %bitcast.7, f32[1,2048]{1,0:T(1,128)} %bitcast.8, s32[1,128]{1,0:T(1,128)} %targets.1, s32[32]{0:T(128)} %domains_hbm.1, ...), custom_call_target="tpu_custom_call" | custom-call | tf_op jit(solution)/shard_map/pallas_call | solution.py:764
  115.3 1.9 %shard_map.104 = (bf16[128,2048]{1,0:T(8,128)(2,1)}, f32[1,128]{1,0:T(1,128)}, f32[7]{0:T(128)}) custom-call(bf16[128,2048]{1,0:T(8,128)(2,1)} %get-tuple-element.8.projected, f32[8,128]{1,0:T(8,128)} %get-tuple-element.9.small), custom_call_target="tpu_custom_call" | custom-call | tf_op jit(solution)/shard_map/pallas_call | solution.py:838

commit v10 on v9

--- a/solution.py
+++ b/solution.py
@@ -606,12 +606,12 @@
         out[some] = (wide * scale * gain[...]).astype(jnp.bfloat16)
         return 0
 
-    lax.fori_loop(0, BLOCK // 16, rows, 0)
+    by_four(rows, BLOCK // 16)
 
 
 def whole_kernel(
-    q_hbm, k_hbm, v_hbm, gain_hbm, targets, domains_hbm, wo_hbm, w_hbm, projected, small,
-    queries, keys, values, gain, domains, qf, kf, probs, numer, state, sums, part, ksum, below, kbelow, above, kabove, cout, kout,
+    q_hbm, k_hbm, v_hbm, gain_hbm, targets, domains_hbm, wo_hbm, w_hbm, projected_hbm, small,
+    queries, keys, values, projected, gain, domains, qf, kf, probs, numer, state, sums, part, ksum, below, kbelow, above, kabove, cout, kout,
     stage, kstage, state_in, sum_in, attended, wo, halves, given, acts, wv, tg, tcol, out_stats, in_stats, dom,
     near, xsend, xrecv, usend, urecv, downsend, downrecv, fsend, frecv, zsend, zrecv, hsend, hrecv, psend, precv,
     gsend, grecv, rsend, rrecv, rprecv, tsend, trecv, ssend, srecv, dsend, drecv,
@@ -734,6 +734,8 @@
         ROW_CUTS, functools.partial(rows_of_event, acts), False, gsend, grecv,
     )
     gather.begin()
+    keep = pltpu.make_async_copy(projected, projected_hbm, near.at[8])
+    keep.start()
     ring.own().wait()
     vocab_part(here, gather, ring, acts, wv, tcol, out_stats, in_stats, ssend, srecv)
     losses = losses_of(here, out_stats, in_stats, ssend, srecv)
@@ -743,6 +745,7 @@
     all_sent(wo.at[0, 0:7, 0], zsend, here)
     prefix.finish_send()
     all_sent(acts.at[0:15, 0:64], psend, here)
+    keep.wait()
     rows_over.wait_send()
     all_sent(given, hsend.at[1], here)
     all_sent(acts.at[0:15], gsend, here)
@@ -768,8 +771,9 @@
             jax.ShapeDtypeStruct((8, BLOCK), wide),
         ),
         in_specs=[anywhere] * 8,
-        out_specs=(vmem, vmem),
+        out_specs=(anywhere, vmem),
         scratch_shapes=[
+            pltpu.VMEM((BLOCK, D), low),
             pltpu.VMEM((BLOCK, D), low),
             pltpu.VMEM((BLOCK, D), low),
             pltpu.VMEM((BLOCK, D), low),
@@ -804,7 +808,7 @@
             pltpu.VMEM((8, 2, 8, 128), wide),
             pltpu.VMEM((2, 16, 8, 128), wide),
             pltpu.VMEM((2, 16, 8, 128), wide),
-            dma((8,)),
+            dma((9,)),
             dma((2,)),
             dma((2,)),
             dma((2,)),

time: 117 us -> 117 us (level)
  no operation moved by 1% of the time
where the time goes in v10:
time: 117 us; the launch traced here: 116 us
  Pallas kernels  116 us (99%)
    pallas_call x1, Pallas kernels, on_device(): pl.pallas_call(whole_kernel, out_shape=(jax.ShapeDtypeStruct((BLOCK, D),...  114 us

profile of v10, /device:TPU:1, one launch (start us, length us, event | category | flops | bytes accessed | tf_op | source)
XLA Modules:
  0.0 116.4 jit_solution(12153538118872684661)
XLA Ops:
  0.6 113.9 %shard_map.103 = (bf16[128,2048]{1,0:T(8,128)(2,1)}, f32[8,128]{1,0:T(8,128)}) custom-call(bf16[128,2048]{1,0:T(8,128)(2,1)} %bitcast.5, bf16[128,2048]{1,0:T(8,128)(2,1)} %bitcast.6, bf16[128,2048]{1,0:T(8,128)(2,1)} %bitcast.7, f32[1,2048]{1,0:T(1,128)} %bitcast.8, s32[1,128]{1,0:T(1,128)} %targets.1, s32[32]{0:T(128)} %domains_hbm.1, ...), custom_call_target="tpu_custom_call" | custom-call | tf_op jit(solution)/shard_map/pallas_call | solution.py:767
  114.6 1.9 %shard_map.104 = (bf16[128,2048]{1,0:T(8,128)(2,1)}, f32[1,128]{1,0:T(1,128)}, f32[7]{0:T(128)}) custom-call(bf16[128,2048]{1,0:T(8,128)(2,1)} %get-tuple-element.8.projected, f32[8,128]{1,0:T(8,128)} %get-tuple-element.9.small), custom_call_target="tpu_custom_call" | custom-call | tf_op jit(solution)/shard_map/pallas_call | solution.py:842
